TPU v7x, 256 devices: a whole 4x4x8 slice. The times are simulated.
256 devices in a mesh: pages: 32 (over x, y, core), mlp: 8 (over z).
Axes of the slice: x: 4, y: 4, z: 8, core: 2. Of those that a mesh axis runs over, the one named last changes fastest.
Arguments:
- embeddings: bfloat16 [8192, 1024], P('pages', 'mlp'), may hold values from -6 to 6
- w_query: bfloat16 [1024, 1024], P(None, 'mlp'), may hold values from -0.1875 to 0.1875
- w_key: bfloat16 [1024, 1024], P(None, 'mlp'), may hold values from -0.1875 to 0.1875
- w_value: bfloat16 [1024, 1024], P(None, 'mlp'), may hold values from -0.1875 to 0.1875
- w_global_query: bfloat16 [1024, 1024], P(None, 'mlp'), may hold values from -0.1875 to 0.1875
- w_out: bfloat16 [1024, 1024], P('mlp'), may hold values from -0.75 to 0.75
- w_up: bfloat16 [1024, 4096], P(None, 'mlp'), may hold values from -0.1875 to 0.1875
- w_down: bfloat16 [4096, 1024], P('mlp'), may hold values from -0.09375 to 0.09375
- norm1_gain: float32 [1024], replicated, may hold values from 0.1 to 1.9
- norm1_bias: float32 [1024], replicated, may hold values from -3 to 3
- norm2_gain: float32 [1024], replicated, may hold values from 0.1 to 1.9
- norm2_bias: float32 [1024], replicated, may hold values from -3 to 3
- cache_keys: bfloat16 [2048, 128, 1024], P('pages', None, 'mlp'), may hold values from -48 to 48
- cache_values: bfloat16 [2048, 128, 1024], P('pages', None, 'mlp'), may hold values from -6 to 6
- lengths: int32 [32], replicated, may hold values from 1 to 8192, as said below
- page_table: int32 [32, 64], replicated, may hold values from -1 to 2047, as said below
- accept: int32 [2, 8192], P(None, 'pages'), may hold values 0 or 1
Outputs:
- refined: bfloat16 [8192, 1024], P('pages', 'mlp')
Inputs may be any that keep to these rules, and one draw needn't show every extreme that they name: `lengths`: one request has exactly 8192 cached tokens. page_table[r, j] is the global slot (holder index times 64 plus local slot) of page j of request r for j < ceil(lengths[r] / 128), and -1 for later j; no slot is named twice; the pages of one request lie on at most 8 page holders, at most 8 on one holder, and the longest request has exactly 8 on each of 8 holders.
All inputs are finite; a program needn't handle non-finite values. No bound on the sum of `accept` on one device may be relied on, other than what follows from the above.
Results may differ from a plain program's by a relative error of at most 0.01.
The roundings to bfloat16 on the way count: a program that leaves them out, or rounds other values in their place, can miss the bound.
Values may be sent and summed in bfloat16 or wider, within the bound.
No kernel may reach another device: no remote copies, remote signals or barrier semaphores. Data moves between devices by JAX's collectives and lax.ppermute only.
A program may use at most 128 MiB of HBM per device.

v0:
```python
import functools

import jax
import jax.numpy as jnp
from jax import lax
from jax.experimental import pallas as pl
from jax.experimental.pallas import tpu as pltpu
from jax.sharding import PartitionSpec as P

HD = 64
BLK = 256
PAGE = 128
EPS = 1e-05
NEG = -1e30
CAP = 2
KEY_BLOCK = 4096
GROUP = 8
PER = 2
LOG2E = 1.4426950408889634
F32 = jnp.float32
BF16 = jnp.bfloat16
VMEM = pl.BlockSpec(memory_space=pltpu.VMEM)
ANY = pl.BlockSpec(memory_space=pl.ANY)
SMEM = pl.BlockSpec(memory_space=pltpu.SMEM)


def routing(page_table, me, holders, slots, hold):
    requests, pages = page_table.shape
    i32 = jnp.int32
    holder_of = jnp.where(page_table >= 0, page_table // slots, -1)
    ids = jnp.arange(holders, dtype=i32)
    page_ids = jnp.arange(pages, dtype=i32)
    on = holder_of[:, None, :] == ids[None, :, None]
    first = jnp.min(jnp.where(on, page_ids[None, None, :], pages), axis=2)
    count = jnp.sum(on.astype(i32), axis=2)
    rank = jnp.sum((first[:, None, :] < first[:, :, None]).astype(i32), axis=2)
    groups = holders // hold
    request_ids = jnp.arange(requests, dtype=i32)
    earlier = request_ids[None, :] < request_ids[:, None]

    def before(sent):
        return jnp.sum((earlier[:, :, None] & sent[None, :, :]).astype(i32), axis=1)

    my_rank = lax.dynamic_slice_in_dim(rank, me, 1, 1)
    my_count = lax.dynamic_slice_in_dim(count, me, 1, 1)
    to = (my_rank % groups == ids[None, :] // hold) & (my_count > ids[None, :] % hold)
    to_turn = before(to)
    mine = holder_of == me
    nth = jnp.sum(
        ((page_ids[None, :, None] > page_ids[None, None, :]) & mine[:, None, :]).astype(i32), axis=2
    )
    local = page_table % slots
    hit = mine[:, None, :] & (nth[:, None, :] == (ids % hold)[None, :, None])
    source = jnp.sum(jnp.where(hit, local[:, None, :], 0), axis=2)

    def send_table(turn):
        want = turn * CAP + jnp.arange(CAP, dtype=i32)
        chosen = to[:, :, None] & (to_turn[:, :, None] == want[None, None, :])
        return jnp.sum(jnp.where(chosen, source[:, :, None], 0), axis=0).reshape(-1)

    places = pages // holders
    came = (rank % groups == me // hold) & (count > me % hold)
    came_turn = before(came)

    def pass_table(turn):
        place = rank // groups
        chosen = (
            came[:, :, None]
            & (place[:, :, None] == jnp.arange(places, dtype=i32)[None, None, :])
            & (came_turn // CAP == turn)[:, :, None]
        )
        origin = ids[None, :] * CAP + came_turn % CAP + 1
        return (jnp.sum(jnp.where(chosen, origin[:, :, None], 0), axis=1) - 1).reshape(-1)

    all_to = (rank[:, :, None] % groups == ids[None, None, :] // hold) & (
        count[:, :, None] > ids[None, None, :] % hold
    )
    rounds = (jnp.max(jnp.sum(all_to.astype(i32), axis=0)) + CAP - 1) // CAP

    own_holder = lax.dynamic_slice_in_dim(holder_of, me, 1, 0)[0]
    own_rank = lax.dynamic_slice_in_dim(rank, me, 1, 0)[0]
    page_rank = jnp.sum(
        jnp.where(own_holder[:, None] == ids[None, :], own_rank[None, :], 0), axis=1
    )
    page_nth = jnp.sum(
        (
            (page_ids[None, :] < page_ids[:, None])
            & (own_holder[None, :] == own_holder[:, None])
        ).astype(i32),
        axis=1,
    )
    unit = page_rank * hold + page_nth
    found = jnp.where(own_holder >= 0, (unit % holders) * places + unit // holders, 0)
    return send_table, pass_table, rounds, found


def staged(total, group, load, stage, packed, got_sem, put_sem):
    for g in range(total // group):
        for i in range(g * group, (g + 1) * group):
            load(i, got_sem.at[g])
    for g in range(total // group):
        part = pl.ds(g * group, group)
        pltpu.make_async_copy(stage.at[part], stage.at[part], got_sem.at[g]).wait()
        pltpu.make_async_copy(stage.at[part], packed.at[part], put_sem).start()
    pltpu.make_async_copy(stage, packed, put_sem).wait()


def pack_kernel(table, keys, values, packed, stage, got_sem, put_sem):
    def load(i, sem):
        slot = table[i]
        pltpu.make_async_copy(keys.at[slot], stage.at[i, 0], sem).start()
        pltpu.make_async_copy(values.at[slot], stage.at[i, 1], sem).start()

    staged(stage.shape[0], GROUP, load, stage, packed, got_sem, put_sem)


def repack_kernel(table, got, packed, stage, got_sem, put_sem):
    def load(i, sem):
        pltpu.make_async_copy(got.at[jnp.maximum(table[i], 0)], stage.at[i], sem).start()

    staged(stage.shape[0], GROUP, load, stage, packed, got_sem, put_sem)


def staged_call(kernel, name, table, page_shape, *arrays):
    shape = (table.shape[0], 2) + page_shape
    return pl.pallas_call(
        kernel,
        out_shape=jax.ShapeDtypeStruct(shape, BF16),
        in_specs=[SMEM] + [ANY] * len(arrays),
        out_specs=ANY,
        scratch_shapes=[
            pltpu.VMEM(shape, BF16),
            pltpu.SemaphoreType.DMA((shape[0] // GROUP,)),
            pltpu.SemaphoreType.DMA,
        ],
        compiler_params=pltpu.CompilerParams(vmem_limit_bytes=60 << 20),
        name=name,
    )(table, *arrays)


def pack_pages(table, keys, values):
    return staged_call(pack_kernel, "pack_pages", table, keys.shape[1:], keys, values)


def repack_pages(table, got):
    return staged_call(repack_kernel, "repack_pages", table, got.shape[2:], got)


def exchange(pages):
    holders = lax.axis_size("pages")
    shape = pages.shape
    sent = lax.all_to_all(
        pages.reshape((holders, shape[0] // holders) + shape[1:]), "pages", 0, 0, tiled=True
    )
    return sent.reshape(shape)


def pages_to_owners(page_table, keys, values, own):
    holders = lax.axis_size("pages")
    me = lax.axis_index("pages")
    hold = 8
    send_table, pass_table, rounds, found = routing(page_table, me, holders, keys.shape[0], hold)
    packed, own = lax.optimization_barrier((pack_pages(send_table(0), keys, values), own))
    x_parts = lax.all_gather(own, "mlp", axis=0)
    first, x_parts = lax.optimization_barrier((exchange(packed), x_parts))
    middle = repack_pages(pass_table(0), first)

    def further(turn, middle):
        got = exchange(pack_pages(send_table(turn), keys, values))
        table = pass_table(turn)
        return jnp.where((table >= 0)[:, None, None, None], repack_pages(table, got), middle)

    middle = lax.fori_loop(1, rounds, further, middle)
    return exchange(middle), found, x_parts


def two_heads(rows):
    lane = lax.broadcasted_iota(jnp.int32, rows.shape, 1)
    low = jnp.where(lane < HD, rows, 0.0)
    high = jnp.where(lane < HD, 0.0, rows)
    return jnp.concatenate([low, high], axis=0).astype(BF16)


def attention_kernel(
    found, length, x_ref, wq, wk, wv, wg, pages, out, x_all, key_buf, value_buf, kept, peak, acc, ksem, vsem
):
    per_block = KEY_BLOCK // PAGE
    shards = x_ref.shape[0]
    width = x_ref.shape[2]
    limit = length[0]
    blocks = (limit + KEY_BLOCK - 1) // KEY_BLOCK

    def block_rows(block):
        return pl.ds(pl.multiple_of(block * KEY_BLOCK, KEY_BLOCK), KEY_BLOCK)

    def fetch(block, carry, part, buf, sem):
        for i in range(per_block):
            page = block * per_block + i
            rows = pl.ds(pl.multiple_of(page * PAGE, PAGE), PAGE)
            pltpu.make_async_copy(pages.at[found[page], part], buf.at[rows], sem.at[block]).start()
        return carry

    lax.fori_loop(0, blocks, functools.partial(fetch, part=0, buf=key_buf, sem=ksem), 0)
    lax.fori_loop(0, blocks, functools.partial(fetch, part=1, buf=value_buf, sem=vsem), 0)
    for i in range(shards):
        x_all[:, i * width : (i + 1) * width] = x_ref[i]
    x = x_all[...]

    def project(matrix):
        return jnp.dot(x, matrix[...], preferred_element_type=F32).astype(BF16)

    scale = HD ** (-0.5)
    queries = two_heads(project(wq).astype(F32) * scale)
    global_rows = two_heads(project(wg).astype(F32) * scale)
    key_rows = project(wk)
    value_rows = project(wv)

    def scores_of(left, keys):
        return lax.dot_general(
            left, keys, (((1,), (1,)), ((), ())), preferred_element_type=F32
        ) * LOG2E

    def fold(scores):
        parts = [scores[:, i : i + 128] for i in range(0, scores.shape[1], 128)]
        while len(parts) > 1:
            parts = [jnp.maximum(*parts[i : i + 2]) for i in range(0, len(parts), 2)]
        return parts[0]

    def weigh(scores, top, values):
        ones = jnp.ones(values.shape, BF16)
        weights = jnp.exp2(scores - top).astype(BF16)
        return jnp.dot(
            weights, jnp.concatenate([values, ones], axis=1), preferred_element_type=F32
        )

    own = scores_of(queries, key_rows)
    peak[...] = fold(own)

    def score_step(block, carry):
        rows = block_rows(block)
        pltpu.make_async_copy(key_buf.at[rows], key_buf.at[rows], ksem.at[block]).wait()
        scores = scores_of(global_rows, key_buf[rows, :])
        position = block * KEY_BLOCK + lax.broadcasted_iota(jnp.int32, scores.shape, 1)
        scores = jnp.where(position < limit, scores, NEG)
        kept[block] = scores
        peak[...] = jnp.maximum(peak[...], fold(scores))
        return carry

    lax.fori_loop(0, blocks, score_step, 0)
    top = jnp.max(peak[...], axis=1, keepdims=True)
    peak[...] = jnp.broadcast_to(top, peak.shape)
    acc[...] = weigh(own, top, value_rows)

    def weigh_step(block, carry):
        rows = block_rows(block)
        pltpu.make_async_copy(value_buf.at[rows], value_buf.at[rows], vsem.at[block]).wait()
        acc[...] += weigh(kept[block], peak[:, :1], value_buf[rows, :])
        return carry

    lax.fori_loop(0, blocks, weigh_step, 0)
    rows = x_ref.shape[1]
    total = acc[...]
    ratio = total[:, :width] / total[:, width:]
    lane = lax.broadcasted_iota(jnp.int32, (rows, width), 1)
    result = jnp.where(lane < HD, ratio[:rows], ratio[rows:]).astype(BF16)
    for i in range(shards):
        out[i] = result


def attend(found, length, x_parts, wq, wk, wv, wg, pages):
    shards, rows, width = x_parts.shape
    longest = found.shape[0] * PAGE
    return pl.pallas_call(
        attention_kernel,
        out_shape=jax.ShapeDtypeStruct(x_parts.shape, BF16),
        in_specs=[SMEM, SMEM, VMEM, VMEM, VMEM, VMEM, VMEM, ANY],
        out_specs=VMEM,
        scratch_shapes=[
            pltpu.VMEM((rows, shards * width), BF16),
            pltpu.VMEM((longest, width), BF16),
            pltpu.VMEM((longest, width), BF16),
            pltpu.VMEM((longest // KEY_BLOCK, 2 * rows, KEY_BLOCK), F32),
            pltpu.VMEM((2 * rows, 128), F32),
            pltpu.VMEM((2 * rows, 2 * width), F32),
            pltpu.SemaphoreType.DMA((longest // KEY_BLOCK,)),
            pltpu.SemaphoreType.DMA((longest // KEY_BLOCK,)),
        ],
        compiler_params=pltpu.CompilerParams(vmem_limit_bytes=56 << 20),
        name="attention",
    )(found, length, x_parts, wq, wk, wv, wg, pages)


def normalize(total, gain, bias, width):
    mean = jnp.sum(total, axis=1, keepdims=True) * (1.0 / width)
    square = jnp.sum(total * total, axis=1, keepdims=True) * (1.0 / width)
    inverse = lax.rsqrt(square - mean * mean + EPS)
    return ((total - mean) * inverse * gain + bias).astype(BF16)


def ffn_kernel(
    att, x_ref, accept, w_out, up_a, up_b, down_a, down_b, g1, b1, g2, b2, out, wide, hidden, acc
):
    step = pl.program_id(0)
    shards, rows, width = x_ref.shape
    full = shards * width

    @pl.when(step == 0)
    def _():
        for i in range(shards):
            wide[:, i * width : (i + 1) * width] = att[i]
        total = jnp.dot(wide[...], w_out[...], preferred_element_type=F32)
        for i in range(shards):
            wide[:, i * width : (i + 1) * width] = x_ref[i]
        total = total + wide[...].astype(F32)
        hidden[...] = normalize(total, g1[...], b1[...], full)
        acc[...] = hidden[...].astype(F32)

    h = hidden[...]
    raised = [
        jnp.dot(h, up[i], preferred_element_type=F32)
        for i in range(up_a.shape[0])
        for up in (up_a, up_b)
    ]
    active = [(0.5 * v * (1.0 + lax.erf(v * (0.5**0.5)))).astype(BF16) for v in raised]
    downs = [down[i] for i in range(up_a.shape[0]) for down in (down_a, down_b)]
    acc[...] += jnp.dot(
        jnp.concatenate(active, axis=1),
        jnp.concatenate(downs, axis=0),
        preferred_element_type=F32,
    )

    @pl.when(step == pl.num_programs(0) - 1)
    def _():
        result = normalize(acc[...], g2[...], b2[...], full)
        chosen = accept[...] != 0
        for i in range(shards):
            out[i] = jnp.where(chosen, result[:, i * width : (i + 1) * width], x_ref[i])


def feed_forward(att, x_parts, accept, w_out, up, down, g1, b1, g2, b2):
    shards, rows, width = x_parts.shape
    full = shards * width

    def fixed(shape):
        return pl.BlockSpec(shape, lambda i: (0,) * len(shape), pipeline_mode=pl.Buffered(1))

    def part(array):
        return pl.BlockSpec((PER,) + array.shape[1:], lambda i: (i, 0, 0))

    return pl.pallas_call(
        ffn_kernel,
        grid=(up[0].shape[0] // PER,),
        out_shape=jax.ShapeDtypeStruct(x_parts.shape, BF16),
        in_specs=[
            fixed(x_parts.shape),
            fixed(x_parts.shape),
            fixed((rows, 1)),
            fixed(w_out.shape),
            part(up[0]),
            part(up[1]),
            part(down[0]),
            part(down[1]),
        ]
        + [fixed((1, full))] * 4,
        out_specs=pl.BlockSpec(x_parts.shape, lambda i: (0, 0, 0)),
        scratch_shapes=[
            pltpu.VMEM((rows, full), BF16),
            pltpu.VMEM((rows, full), BF16),
            pltpu.VMEM((rows, full), F32),
        ],
        compiler_params=pltpu.CompilerParams(
            dimension_semantics=("arbitrary",), vmem_limit_bytes=60 << 20
        ),
        name="feed_forward",
    )(att, x_parts, accept, w_out, up[0], up[1], down[0], down[1], g1, b1, g2, b2)


def to_all(copies):
    return lax.all_to_all(copies, "mlp", 0, 0, tiled=True)


def core_pair():
    return [(i, i ^ 1) for i in range(lax.axis_size("pages"))]


def per_device(
    embeddings,
    w_query,
    w_key,
    w_value,
    w_global_query,
    w_out,
    w_up,
    w_down,
    norm1_gain,
    norm1_bias,
    norm2_gain,
    norm2_bias,
    cache_keys,
    cache_values,
    lengths,
    page_table,
    accept,
):
    shards = lax.axis_size("mlp")
    me = lax.axis_index("pages")
    shard = lax.axis_index("mlp")
    rows, width = embeddings.shape
    pages, found, x_parts = pages_to_owners(page_table, cache_keys, cache_values, embeddings)
    length = lax.dynamic_slice_in_dim(lengths, me, 1, 0)

    core = me % 2
    half = w_up.shape[1] // 2
    up_half = lax.dynamic_slice_in_dim(w_up, core * half, half, 1)
    down_half = lax.dynamic_slice_in_dim(w_down, core * half, half, 0)
    w_out_all = lax.all_gather(w_out, "mlp", axis=0, tiled=True)
    up_mine = lax.all_gather(up_half, "mlp", axis=0)
    down_mine = lax.all_gather(down_half, "mlp", axis=0)
    up_other = lax.ppermute(up_mine, "pages", core_pair())
    down_other = lax.ppermute(down_mine, "pages", core_pair())
    norms = [v.reshape(1, -1) for v in (norm1_gain, norm1_bias, norm2_gain, norm2_bias)]

    for pass_index in range(2):
        attention = attend(
            found, length, x_parts, w_query, w_key, w_value, w_global_query, pages
        )
        x_parts = feed_forward(
            to_all(attention),
            x_parts,
            accept[pass_index].reshape(rows, 1),
            w_out_all,
            (up_mine, up_other),
            (down_mine, down_other),
            *norms,
        )
    return lax.dynamic_index_in_dim(x_parts, shard, 0, keepdims=False)


def solution(mesh):
    return jax.shard_map(
        per_device,
        mesh=mesh,
        in_specs=(
            P("pages", "mlp"),
            P(None, "mlp"),
            P(None, "mlp"),
            P(None, "mlp"),
            P(None, "mlp"),
            P("mlp", None),
            P(None, "mlp"),
            P("mlp", None),
            P(),
            P(),
            P(),
            P(),
            P("pages", None, "mlp"),
            P("pages", None, "mlp"),
            P(),
            P(),
            P(None, "pages"),
        ),
        out_specs=P("pages", "mlp"),
        check_vma=False,
    )
```

profile of v0, /device:TPU:9, one launch (start us, length us, event | category | flops | bytes accessed | tf_op | source)
XLA Modules:
  0.0 250.6 jit_solution(12320336003428784115)
XLA Ops:
  6.5 0.0 copy-start
  6.5 0.0 all-gather.9.cloned.1.call-start
  6.5 1.2 copy-done
  7.8 0.9 constant_dynamic-slice_fusion.1
  8.6 0.0 all-gather.9.cloned.1.call-update
  8.7 0.7 broadcast_compare_fusion.1
  9.4 1.2 convert_reduce_fusion.4
  10.6 0.8 convert_reduce_fusion.5
  11.4 0.2 fusion.19
  11.6 0.6 convert_reduce_fusion
  12.2 0.1 compare_and_fusion.2
  12.3 0.3 convert_reduce_fusion.2
  12.6 0.7 add_select_fusion.7
  13.3 0.7 select_reduce_fusion.2
  14.1 0.1 copy.24
  14.2 0.6 reshape.570.table
  14.8 6.5 %pack_pages.7 = bf16[64,2,128,128]{3,2,1,0:T(8,128)(2,1)} custom-call(s32[64]{0:T(128)} %reshape.570.table, bf16[64,128,128]{2,1,0:T(8,128)(2,1)} %keys.1, bf16[64,128,128]{2,1,0:T(8,128)(2,1)} %values.1), custom_call_target="tpu_custom_call" | custom-call | tf_op jit(solution)/shard_map/pack_pages/pallas_call | solution.py:126
  21.3 0.0 copy-start.4
  21.3 0.0 copy-start.5
  21.4 8.1 %all-to-all-start.1 = ((bf16[32,2,2,128,128]{4,3,2,1,0:T(8,128)(2,1)}), bf16[32,2,2,128,128]{4,3,2,1,0:T(8,128)(2,1)}, u32[]{:S(2)}, u32[]{:S(2)}) async-start(bf16[32,2,2,128,128]{4,3,2,1,0:T(8,128)(2,1)} %bitcast.59), calls=%async_computation.1 | async-start | bytes 8388608 | tf_op jit(solution)/shard_map/all_to_all | solution.py:152
  29.5 0.0 all-gather.11.cloned.1.call-start
  29.5 0.0 copy-done.4
  29.6 0.9 constant_dynamic-slice_fusion
  30.5 0.0 all-gather.11.cloned.1.call-update
  30.5 0.3 convert_reduce_fusion.1
  30.9 0.6 reduce_max.9
  32.2 0.1 select_reduce_fusion.4
  32.3 0.1 copy.25
  32.4 0.7 sub.71.table
  33.1 0.0 copy-done.5
  33.1 28.6 %all-gather = bf16[2048,128]{1,0:T(8,128)(2,1)} all-gather(bf16[256,128]{1,0:T(8,128)(2,1)S(1)} %copy-done.5), channel_id=2, replica_groups=mesh['pages'=32,'mlp'=8] {'mlp'}, dimensions={0}, use_global_device_ids=true | all-gather | bytes 589824 | tf_op jit(solution)/shard_map/all_gather | solution.py:164
  61.8 21.8 %all-to-all-done.1 = bf16[32,2,2,128,128]{4,3,2,1,0:T(8,128)(2,1)} async-done(((bf16[32,2,2,128,128]{4,3,2,1,0:T(8,128)(2,1)}), bf16[32,2,2,128,128]{4,3,2,1,0:T(8,128)(2,1)}, u32[]{:S(2)}, u32[]{:S(2)}) %all-to-all-start.1) | async-done | bytes 4194336 | tf_op jit(solution)/shard_map/all_to_all | solution.py:152
  83.5 5.5 %repack_pages.7 = bf16[64,2,128,128]{3,2,1,0:T(8,128)(2,1)} custom-call(s32[64]{0:T(128)} %sub.71.table, bf16[64,2,128,128]{3,2,1,0:T(8,128)(2,1)} %bitcast.3.got), custom_call_target="tpu_custom_call" | custom-call | tf_op jit(solution)/shard_map/repack_pages/pallas_call | solution.py:126
  89.1 0.0 copy-done.1
  89.1 0.0 copy-start.8
  89.1 6.7 %all-to-all-start.2 = ((bf16[32,2,2,128,128]{4,3,2,1,0:T(8,128)(2,1)}), bf16[32,2,2,128,128]{4,3,2,1,0:T(8,128)(2,1)}, u32[]{:S(2)}, u32[]{:S(2)}) async-start(bf16[32,2,2,128,128]{4,3,2,1,0:T(8,128)(2,1)} %bitcast.58), calls=%async_computation.2 | async-start | bytes 8388608 | tf_op jit(solution)/shard_map/all_to_all | solution.py:152
  95.8 0.0 copy-start.7
  95.9 0.0 all-gather.7.cloned.1.call-start
  95.9 0.0 all-gather.9.cloned.1.call-done
  95.9 0.4 collective-permute-start
  96.4 30.7 %all-gather.11.cloned.1.call-done = bf16[2048,1024]{1,0:T(8,128)(2,1)} async-done(((bf16[256,1024]{1,0:T(8,128)(2,1)}), bf16[2048,1024]{1,0:T(8,128)(2,1)}) %all-gather.11.cloned.1.call-update) | async-done | bytes 4194320 | tf_op jit(solution)/shard_map/all_gather | solution.py:418
  127.0 0.7 collective-permute-start.1
  127.7 0.0 all-gather.7.cloned.1.call-update
  127.7 0.6 dynamic_slice.29.length
  128.4 0.2 convert_reduce_fusion.6
  128.6 0.1 select_reduce_fusion.6
  128.6 0.5 compare_select_fusion.1.found
  129.2 20.7 %all-to-all-done.2 = bf16[32,2,2,128,128]{4,3,2,1,0:T(8,128)(2,1)} async-done(((bf16[32,2,2,128,128]{4,3,2,1,0:T(8,128)(2,1)}), bf16[32,2,2,128,128]{4,3,2,1,0:T(8,128)(2,1)}, u32[]{:S(2)}, u32[]{:S(2)}) %all-to-all-start.2) | async-done | bytes 4194336 | tf_op jit(solution)/shard_map/all_to_all | solution.py:152
  149.9 10.0 %attention.2 = bf16[8,256,128]{2,1,0:T(8,128)(2,1)} custom-call(s32[64]{0:T(128)} %compare_select_fusion.1.found, s32[1]{0:T(128)} %dynamic_slice.29.length, bf16[8,256,128]{2,1,0:T(8,128)(2,1)} %bitcast.66, bf16[1024,128]{1,0:T(8,128)(2,1)} %wq.3, bf16[1024,128]{1,0:T(8,128)(2,1)} %wk.3, bf16[1024,128]{1,0:T(8,128)(2,1)} %wv.3, bf16[1024,128]{1,0:T(8,128)(2,1)} %wg.3, ...), custom_call_target="tpu_custom_call" | custom-call | tf_op jit(solution)/shard_map/attention/pallas_call | solution.py:273
  159.9 8.2 %all-to-all-start.3 = ((bf16[8,256,128]{2,1,0:T(8,128)(2,1)}), bf16[8,256,128]{2,1,0:T(8,128)(2,1)S(1)}, u32[]{:S(2)}, u32[]{:S(2)}) async-start(bf16[8,256,128]{2,1,0:T(8,128)(2,1)} %attention.2), calls=%async_computation.3 | async-start | bytes 1048576 | tf_op jit(solution)/shard_map/all_to_all | solution.py:379
  168.0 0.0 copy-done.7
  168.1 0.8 copy.26.accept
  168.9 16.8 %all-to-all-done.3.att = bf16[8,256,128]{2,1,0:T(8,128)(2,1)S(1)} async-done(((bf16[8,256,128]{2,1,0:T(8,128)(2,1)}), bf16[8,256,128]{2,1,0:T(8,128)(2,1)S(1)}, u32[]{:S(2)}, u32[]{:S(2)}) %all-to-all-start.3) | async-done | bytes 524320 | tf_op jit(solution)/shard_map/all_to_all | solution.py:379
  185.6 0.0 collective-permute-done.up_b
  185.6 0.0 collective-permute-done.1.down_b
  185.6 0.8 copy-done.3
  186.4 12.0 %feed_forward.2.x_ref = bf16[8,256,128]{2,1,0:T(8,128)(2,1)} custom-call(bf16[8,256,128]{2,1,0:T(8,128)(2,1)} %copy-done.3, bf16[8,256,128]{2,1,0:T(8,128)(2,1)} %bitcast.67, s32[256,1]{1,0:T(8,128)} %copy.26.accept, bf16[1024,1024]{1,0:T(8,128)(2,1)} %all-gather.7.cloned.1.call-done.w_out, bf16[8,1024,256]{2,1,0:T(8,128)(2,1)} %bitcast.61, ...), custom_call_target="tpu_custom_call" | custom-call | tf_op jit(solution)/shard_map/feed_forward/pallas_call | solution.py:350
  198.5 9.8 %attention.3 = bf16[8,256,128]{2,1,0:T(8,128)(2,1)} custom-call(s32[64]{0:T(128)} %compare_select_fusion.1.found, s32[1]{0:T(128)} %dynamic_slice.29.length, bf16[8,256,128]{2,1,0:T(8,128)(2,1)} %feed_forward.2.x_ref, bf16[1024,128]{1,0:T(8,128)(2,1)} %wq.3, bf16[1024,128]{1,0:T(8,128)(2,1)} %wk.3, bf16[1024,128]{1,0:T(8,128)(2,1)} %wv.3, ...), custom_call_target="tpu_custom_call" | custom-call | tf_op jit(solution)/shard_map/attention/pallas_call | solution.py:273
  208.3 3.5 %all-to-all-start.4 = ((bf16[8,256,128]{2,1,0:T(8,128)(2,1)}), bf16[8,256,128]{2,1,0:T(8,128)(2,1)S(1)}, u32[]{:S(2)}, u32[]{:S(2)}) async-start(bf16[8,256,128]{2,1,0:T(8,128)(2,1)} %attention.3), calls=%async_computation.4 | async-start | bytes 1048576 | tf_op jit(solution)/shard_map/all_to_all | solution.py:379
  211.8 0.8 copy.27.accept
  212.6 17.1 %all-to-all-done.4.att = bf16[8,256,128]{2,1,0:T(8,128)(2,1)S(1)} async-done(((bf16[8,256,128]{2,1,0:T(8,128)(2,1)}), bf16[8,256,128]{2,1,0:T(8,128)(2,1)S(1)}, u32[]{:S(2)}, u32[]{:S(2)}) %all-to-all-start.4) | async-done | bytes 524320 | tf_op jit(solution)/shard_map/all_to_all | solution.py:379
  229.7 0.8 copy-done.2
  230.5 12.1 %feed_forward.3 = bf16[8,256,128]{2,1,0:T(8,128)(2,1)} custom-call(bf16[8,256,128]{2,1,0:T(8,128)(2,1)} %copy-done.2, bf16[8,256,128]{2,1,0:T(8,128)(2,1)} %feed_forward.2.x_ref, s32[256,1]{1,0:T(8,128)} %copy.27.accept, bf16[1024,1024]{1,0:T(8,128)(2,1)} %all-gather.7.cloned.1.call-done.w_out, bf16[8,1024,256]{2,1,0:T(8,128)(2,1)} %bitcast.62, ...), custom_call_target="tpu_custom_call" | custom-call | tf_op jit(solution)/shard_map/feed_forward/pallas_call | solution.py:350
  242.6 1.5 dynamic-slice_bitcast_fusion
  (18 shorter events, 0.2 us)
Async XLA Ops:
  6.5 1.2 copy-start
  6.5 89.4 %all-gather.9.cloned.1.call-start = ((), (), s32[]{:S(2)}) async-start(), calls=%async_computation.6 | async-start | bytes 4718592 | tf_op jit(solution)/shard_map/all_gather | solution.py:417
  21.3 8.2 %copy-start.4 = (bf16[512,1024]{1,0:T(8,128)(2,1)S(1)}, bf16[512,1024]{1,0:T(8,128)(2,1)}, u32[]{:S(2)}) copy-start(bf16[512,1024]{1,0:T(8,128)(2,1)} %param.26) | copy-start | bytes 3145732
  21.3 11.8 %copy-start.5 = (bf16[256,128]{1,0:T(8,128)(2,1)S(1)}, bf16[256,128]{1,0:T(8,128)(2,1)}, u32[]{:S(2)}) copy-start(bf16[256,128]{1,0:T(8,128)(2,1)} %param.19) | copy-start | bytes 196612
  21.4 62.2 %all-to-all-start.1 = ((bf16[32,2,2,128,128]{4,3,2,1,0:T(8,128)(2,1)}), bf16[32,2,2,128,128]{4,3,2,1,0:T(8,128)(2,1)}, u32[]{:S(2)}, u32[]{:S(2)}) async-start(bf16[32,2,2,128,128]{4,3,2,1,0:T(8,128)(2,1)} %bitcast.59), calls=%async_computation.1 | async-start | bytes 8388608 | tf_op jit(solution)/shard_map/all_to_all | solution.py:152
  29.5 97.5 %all-gather.11.cloned.1.call-start = ((), (), s32[]{:S(2)}) async-start(), calls=%async_computation.7 | async-start | bytes 4718592 | tf_op jit(solution)/shard_map/all_gather | solution.py:418
  83.5 5.5 %copy-start.1 = (bf16[64,128,128]{2,1,0:T(8,128)(2,1)S(1)}, bf16[64,128,128]{2,1,0:T(8,128)(2,1)}, u32[]{:S(2)}) copy-start(bf16[64,128,128]{2,1,0:T(8,128)(2,1)} %keys.1) | copy-start | bytes 6291460
  89.1 38.7 %copy-start.8 = (s32[32]{0:T(128)S(1)}, s32[32]{0:T(128)}, u32[]{:S(2)}) copy-start(s32[32]{0:T(128)} %param.33) | copy-start | bytes 388
  89.1 60.8 %all-to-all-start.2 = ((bf16[32,2,2,128,128]{4,3,2,1,0:T(8,128)(2,1)}), bf16[32,2,2,128,128]{4,3,2,1,0:T(8,128)(2,1)}, u32[]{:S(2)}, u32[]{:S(2)}) async-start(bf16[32,2,2,128,128]{4,3,2,1,0:T(8,128)(2,1)} %bitcast.58), calls=%async_computation.2 | async-start | bytes 8388608 | tf_op jit(solution)/shard_map/all_to_all | solution.py:152
  95.8 72.2 %copy-start.7 = (s32[2,256]{1,0:T(2,128)S(1)}, s32[2,256]{1,0:T(2,128)}, u32[]{:S(2)}) copy-start(s32[2,256]{1,0:T(2,128)} %param.35) | copy-start | bytes 6148
  95.9 73.0 %all-gather.7.cloned.1.call-start = ((), (), s32[]{:S(2)}) async-start(), calls=%async_computation.5 | async-start | bytes 2359296 | tf_op jit(solution)/shard_map/all_gather | solution.py:416
  95.9 89.7 %collective-permute-start = (bf16[8,1024,256]{2,1,0:T(8,128)(2,1)}, bf16[8,1024,256]{2,1,0:T(8,128)(2,1)}, u32[]{:S(2)}, u32[]{:S(2)}) collective-permute-start(bf16[8,1024,256]{2,1,0:T(8,128)(2,1)} %bitcast.60), channel_id=1, source_target_pairs={{0,8},{8,0},{16,24},{24,16},{32,40},{40,32},{48,56},{56,48},{64,72... | collective-permute-start | bytes 12582920 | tf_op jit(solution)/shard_map/ppermute | solution.py:419
  127.0 58.6 %collective-permute-start.1 = (bf16[8,256,1024]{2,1,0:T(8,128)(2,1)}, bf16[8,256,1024]{2,1,0:T(8,128)(2,1)}, u32[]{:S(2)}, u32[]{:S(2)}) collective-permute-start(bf16[8,256,1024]{2,1,0:T(8,128)(2,1)} %bitcast.63), channel_id=1, source_target_pairs={{0,8},{8,0},{16,24},{24,16},{32,40},{40,32},{48,56},{56,48},{64,72... | collective-permute-start | bytes 12582920 | tf_op jit(solution)/shard_map/ppermute | solution.py:420
  159.9 25.8 %all-to-all-start.3 = ((bf16[8,256,128]{2,1,0:T(8,128)(2,1)}), bf16[8,256,128]{2,1,0:T(8,128)(2,1)S(1)}, u32[]{:S(2)}, u32[]{:S(2)}) async-start(bf16[8,256,128]{2,1,0:T(8,128)(2,1)} %attention.2), calls=%async_computation.3 | async-start | bytes 1048576 | tf_op jit(solution)/shard_map/all_to_all | solution.py:379
  185.6 0.8 copy-start.3
  208.3 21.4 %all-to-all-start.4 = ((bf16[8,256,128]{2,1,0:T(8,128)(2,1)}), bf16[8,256,128]{2,1,0:T(8,128)(2,1)S(1)}, u32[]{:S(2)}, u32[]{:S(2)}) async-start(bf16[8,256,128]{2,1,0:T(8,128)(2,1)} %attention.3), calls=%async_computation.4 | async-start | bytes 1048576 | tf_op jit(solution)/shard_map/all_to_all | solution.py:379
  229.7 0.8 copy-start.2
Sparse Core Ops, SparseCore 0:
  9.1 62.6 all-gather.8
  73.6 53.4 all-gather.10
  128.8 35.9 all-gather.6
where the time goes:
time: 250 us; the launch traced here: 251 us
  waiting for transfers between devices  107 us (43%)
  Pallas kernels  56 us (22%)
  blocking collectives  28.6 us (11%)
  starting transfers between devices  27.8 us (11%)
  between operations  14 us (6%)
  local copies, waits for them, and re-layouts  9.83 us (4%)
  other arithmetic  7.29 us (3%)
    all_to_all x2, waiting for transfers between devices, exchange(): lax.all_to_all(pages.reshape((holders, shape[0] // holders) + shape[1:]),...  42.5 us
    all_to_all x2, waiting for transfers between devices, to_all(): return lax.all_to_all(copies, 'mlp', 0, 0, tiled=True)  33.8 us
    all_gather x1, waiting for transfers between devices, per_device(): down_mine = lax.all_gather(down_half, 'mlp', axis=0)  30.7 us
    all_gather x1, blocking collectives, pages_to_owners(): x_parts = lax.all_gather(own, 'mlp', axis=0)  28.6 us
    pallas_call x2, Pallas kernels, feed_forward(): pl.pallas_call(ffn_kernel, grid=(up[0].shape[0] // PER,), out_shape=jax.S...  24.1 us
    pallas_call x2, Pallas kernels, attend(): pl.pallas_call(attention_kernel, out_shape=jax.ShapeDtypeStruct(x_parts.s...  19.8 us
    all_to_all x2, starting transfers between devices, exchange(): lax.all_to_all(pages.reshape((holders, shape[0] // holders) + shape[1:]),...  14.9 us
    pallas_call x2, Pallas kernels, staged_call(): pl.pallas_call(kernel, out_shape=jax.ShapeDtypeStruct(shape, BF16), in_sp...  12.1 us
  transfers between devices with their start and end apart: 9, of which 5 were waited for; matrix products, arithmetic and copies ran while one was open for 5% of the time, Pallas kernels for 9%

commit v1 on v0

--- a/solution.py
+++ b/solution.py
@@ -15,6 +15,7 @@
 CAP = 2
 KEY_BLOCK = 4096
 GROUP = 8
+HOLD = 8
 PER = 2
 LOG2E = 1.4426950408889634
 F32 = jnp.float32
@@ -41,23 +42,6 @@
     def before(sent):
         return jnp.sum((earlier[:, :, None] & sent[None, :, :]).astype(i32), axis=1)
 
-    my_rank = lax.dynamic_slice_in_dim(rank, me, 1, 1)
-    my_count = lax.dynamic_slice_in_dim(count, me, 1, 1)
-    to = (my_rank % groups == ids[None, :] // hold) & (my_count > ids[None, :] % hold)
-    to_turn = before(to)
-    mine = holder_of == me
-    nth = jnp.sum(
-        ((page_ids[None, :, None] > page_ids[None, None, :]) & mine[:, None, :]).astype(i32), axis=2
-    )
-    local = page_table % slots
-    hit = mine[:, None, :] & (nth[:, None, :] == (ids % hold)[None, :, None])
-    source = jnp.sum(jnp.where(hit, local[:, None, :], 0), axis=2)
-
-    def send_table(turn):
-        want = turn * CAP + jnp.arange(CAP, dtype=i32)
-        chosen = to[:, :, None] & (to_turn[:, :, None] == want[None, None, :])
-        return jnp.sum(jnp.where(chosen, source[:, :, None], 0), axis=0).reshape(-1)
-
     places = pages // holders
     came = (rank % groups == me // hold) & (count > me % hold)
     came_turn = before(came)
@@ -91,7 +75,7 @@
     )
     unit = page_rank * hold + page_nth
     found = jnp.where(own_holder >= 0, (unit % holders) * places + unit // holders, 0)
-    return send_table, pass_table, rounds, found
+    return pass_table, rounds, found
 
 
 def staged(total, group, load, stage, packed, got_sem, put_sem):
@@ -105,9 +89,57 @@
     pltpu.make_async_copy(stage, packed, put_sem).wait()
 
 
-def pack_kernel(table, keys, values, packed, stage, got_sem, put_sem):
+def pack_kernel(
+    where_and_turn, page_table, keys, values, packed, table_v, table, stage, table_sem, got_sem, put_sem
+):
+    me, turn = where_and_turn[0], where_and_turn[1]
+    requests, pages = page_table.shape
+    slots = keys.shape[0]
+    holders = packed.shape[0] // CAP
+    groups = holders // HOLD
+    i32 = jnp.int32
+    slot_of = page_table[...]
+    holder_of = jnp.where(slot_of >= 0, slot_of // slots, -1)
+    local = slot_of % slots
+    page_ids = lax.broadcasted_iota(i32, slot_of.shape, 1)
+    mine = holder_of == me
+
+    def first_of(on):
+        return jnp.min(jnp.where(on, page_ids, pages), axis=1, keepdims=True)
+
+    own_first = first_of(mine)
+    rank = jnp.zeros((requests, 1), i32)
+    for holder in range(holders):
+        rank += (first_of(holder_of == holder) < own_first).astype(i32)
+    mine_f = mine.astype(F32)
+    count = jnp.sum(mine_f, axis=1, keepdims=True).astype(i32)
+    before = lax.broadcasted_iota(i32, (pages, pages), 0) < lax.broadcasted_iota(
+        i32, (pages, pages), 1
+    )
+    nth = jnp.dot(mine_f, before.astype(F32), preferred_element_type=F32).astype(i32)
+    target = lax.broadcasted_iota(i32, (requests, holders), 1)
+    to = (rank % groups == target // HOLD) & (count > target % HOLD)
+    source = jnp.zeros((requests, holders), i32)
+    for k in range(HOLD):
+        hit = jnp.sum(jnp.where(mine & (nth == k), local, 0), axis=1, keepdims=True)
+        source = jnp.where(target % HOLD == k, hit, source)
+    earlier = lax.broadcasted_iota(i32, (requests, requests), 1) < lax.broadcasted_iota(
+        i32, (requests, requests), 0
+    )
+    order = jnp.dot(
+        earlier.astype(F32), to.astype(F32), preferred_element_type=F32
+    ).astype(i32)
+    for place in range(CAP):
+        chosen = to & (order == turn * CAP + place)
+        table_v[place : place + 1, 0:holders] = jnp.sum(
+            jnp.where(chosen, source, 0), axis=0, keepdims=True
+        )
+    copy = pltpu.make_async_copy(table_v, table, table_sem)
+    copy.start()
+    copy.wait()
+
     def load(i, sem):
-        slot = table[i]
+        slot = table[i % CAP, i // CAP]
         pltpu.make_async_copy(keys.at[slot], stage.at[i, 0], sem).start()
         pltpu.make_async_copy(values.at[slot], stage.at[i, 1], sem).start()
 
@@ -121,29 +153,43 @@
     staged(stage.shape[0], GROUP, load, stage, packed, got_sem, put_sem)
 
 
-def staged_call(kernel, name, table, page_shape, *arrays):
-    shape = (table.shape[0], 2) + page_shape
+def staging(shape):
+    return [
+        pltpu.VMEM(shape, BF16),
+        pltpu.SemaphoreType.DMA((shape[0] // GROUP,)),
+        pltpu.SemaphoreType.DMA,
+    ]
+
+
+def pack_pages(me, turn, page_table, keys, values):
+    shape = (lax.axis_size("pages") * CAP, 2) + keys.shape[1:]
     return pl.pallas_call(
-        kernel,
+        pack_kernel,
         out_shape=jax.ShapeDtypeStruct(shape, BF16),
-        in_specs=[SMEM] + [ANY] * len(arrays),
+        in_specs=[SMEM, VMEM, ANY, ANY],
         out_specs=ANY,
         scratch_shapes=[
-            pltpu.VMEM(shape, BF16),
-            pltpu.SemaphoreType.DMA((shape[0] // GROUP,)),
+            pltpu.VMEM((8, 128), jnp.int32),
+            pltpu.SMEM((8, 128), jnp.int32),
+            staging(shape)[0],
             pltpu.SemaphoreType.DMA,
-        ],
+        ]
+        + staging(shape)[1:],
         compiler_params=pltpu.CompilerParams(vmem_limit_bytes=60 << 20),
-        name=name,
-    )(table, *arrays)
-
-
-def pack_pages(table, keys, values):
-    return staged_call(pack_kernel, "pack_pages", table, keys.shape[1:], keys, values)
+        name="pack_pages",
+    )(jnp.stack([me, turn]).astype(jnp.int32), page_table, keys, values)
 
 
 def repack_pages(table, got):
-    return staged_call(repack_kernel, "repack_pages", table, got.shape[2:], got)
+    return pl.pallas_call(
+        repack_kernel,
+        out_shape=jax.ShapeDtypeStruct(got.shape, BF16),
+        in_specs=[SMEM, ANY],
+        out_specs=ANY,
+        scratch_shapes=staging(got.shape),
+        compiler_params=pltpu.CompilerParams(vmem_limit_bytes=60 << 20),
+        name="repack_pages",
+    )(table, got)
 
 
 def exchange(pages):
@@ -155,23 +201,24 @@
     return sent.reshape(shape)
 
 
-def pages_to_owners(page_table, keys, values, own):
+def pages_to_owners(page_table, keys, values, later):
     holders = lax.axis_size("pages")
     me = lax.axis_index("pages")
-    hold = 8
-    send_table, pass_table, rounds, found = routing(page_table, me, holders, keys.shape[0], hold)
-    packed, own = lax.optimization_barrier((pack_pages(send_table(0), keys, values), own))
-    x_parts = lax.all_gather(own, "mlp", axis=0)
+    packed, table, later = lax.optimization_barrier(
+        (pack_pages(me, 0, page_table, keys, values), page_table, later)
+    )
+    pass_table, rounds, found = routing(table, me, holders, keys.shape[0], HOLD)
+    x_parts = lax.all_gather(later[0], "mlp", axis=0)
     first, x_parts = lax.optimization_barrier((exchange(packed), x_parts))
     middle = repack_pages(pass_table(0), first)
 
     def further(turn, middle):
-        got = exchange(pack_pages(send_table(turn), keys, values))
+        got = exchange(pack_pages(me, turn, page_table, keys, values))
         table = pass_table(turn)
         return jnp.where((table >= 0)[:, None, None, None], repack_pages(table, got), middle)
 
     middle = lax.fori_loop(1, rounds, further, middle)
-    return exchange(middle), found, x_parts
+    return exchange(middle), found, x_parts, later[1:]
 
 
 def two_heads(rows):
@@ -181,12 +228,55 @@
     return jnp.concatenate([low, high], axis=0).astype(BF16)
 
 
+def project_kernel(x_ref, wq, wk, wv, wg, queries, global_rows, key_rows, value_rows, x_all):
+    shards, _, width = x_ref.shape
+    for i in range(shards):
+        x_all[:, i * width : (i + 1) * width] = x_ref[i]
+    x = x_all[...]
+
+    def project(matrix):
+        return jnp.dot(x, matrix[...], preferred_element_type=F32).astype(BF16)
+
+    scale = HD ** (-0.5)
+    queries[...] = two_heads(project(wq).astype(F32) * scale)
+    global_rows[...] = two_heads(project(wg).astype(F32) * scale)
+    key_rows[...] = project(wk)
+    value_rows[...] = project(wv)
+
+
+def project_all(x_parts, wq, wk, wv, wg):
+    shards, rows, width = x_parts.shape
+    doubled = jax.ShapeDtypeStruct((2 * rows, width), BF16)
+    single = jax.ShapeDtypeStruct((rows, width), BF16)
+    return pl.pallas_call(
+        project_kernel,
+        out_shape=(doubled, doubled, single, single),
+        in_specs=[VMEM] * 5,
+        out_specs=(VMEM,) * 4,
+        scratch_shapes=[pltpu.VMEM((rows, shards * width), BF16)],
+        name="project",
+    )(x_parts, wq, wk, wv, wg)
+
+
 def attention_kernel(
-    found, length, x_ref, wq, wk, wv, wg, pages, out, x_all, key_buf, value_buf, kept, peak, acc, ksem, vsem
+    found,
+    length,
+    queries,
+    global_rows,
+    key_rows,
+    value_rows,
+    pages,
+    out,
+    key_buf,
+    value_buf,
+    kept,
+    peak,
+    acc,
+    ksem,
+    vsem,
 ):
     per_block = KEY_BLOCK // PAGE
-    shards = x_ref.shape[0]
-    width = x_ref.shape[2]
+    shards, rows, width = out.shape
     limit = length[0]
     blocks = (limit + KEY_BLOCK - 1) // KEY_BLOCK
 
@@ -202,19 +292,6 @@
 
     lax.fori_loop(0, blocks, functools.partial(fetch, part=0, buf=key_buf, sem=ksem), 0)
     lax.fori_loop(0, blocks, functools.partial(fetch, part=1, buf=value_buf, sem=vsem), 0)
-    for i in range(shards):
-        x_all[:, i * width : (i + 1) * width] = x_ref[i]
-    x = x_all[...]
-
-    def project(matrix):
-        return jnp.dot(x, matrix[...], preferred_element_type=F32).astype(BF16)
-
-    scale = HD ** (-0.5)
-    queries = two_heads(project(wq).astype(F32) * scale)
-    global_rows = two_heads(project(wg).astype(F32) * scale)
-    key_rows = project(wk)
-    value_rows = project(wv)
-
     def scores_of(left, keys):
         return lax.dot_general(
             left, keys, (((1,), (1,)), ((), ())), preferred_element_type=F32
@@ -233,13 +310,13 @@
             weights, jnp.concatenate([values, ones], axis=1), preferred_element_type=F32
         )
 
-    own = scores_of(queries, key_rows)
+    own = scores_of(queries[...], key_rows[...])
     peak[...] = fold(own)
 
     def score_step(block, carry):
-        rows = block_rows(block)
-        pltpu.make_async_copy(key_buf.at[rows], key_buf.at[rows], ksem.at[block]).wait()
-        scores = scores_of(global_rows, key_buf[rows, :])
+        part = key_buf.at[block_rows(block)]
+        pltpu.make_async_copy(part, part, ksem.at[block]).wait()
+        scores = scores_of(global_rows[...], key_buf[block_rows(block), :])
         position = block * KEY_BLOCK + lax.broadcasted_iota(jnp.int32, scores.shape, 1)
         scores = jnp.where(position < limit, scores, NEG)
         kept[block] = scores
@@ -249,16 +326,15 @@
     lax.fori_loop(0, blocks, score_step, 0)
     top = jnp.max(peak[...], axis=1, keepdims=True)
     peak[...] = jnp.broadcast_to(top, peak.shape)
-    acc[...] = weigh(own, top, value_rows)
+    acc[...] = weigh(own, top, value_rows[...])
 
     def weigh_step(block, carry):
-        rows = block_rows(block)
-        pltpu.make_async_copy(value_buf.at[rows], value_buf.at[rows], vsem.at[block]).wait()
-        acc[...] += weigh(kept[block], peak[:, :1], value_buf[rows, :])
+        part = value_buf.at[block_rows(block)]
+        pltpu.make_async_copy(part, part, vsem.at[block]).wait()
+        acc[...] += weigh(kept[block], peak[:, :1], value_buf[block_rows(block), :])
         return carry
 
     lax.fori_loop(0, blocks, weigh_step, 0)
-    rows = x_ref.shape[1]
     total = acc[...]
     ratio = total[:, :width] / total[:, width:]
     lane = lax.broadcasted_iota(jnp.int32, (rows, width), 1)
@@ -267,16 +343,15 @@
         out[i] = result
 
 
-def attend(found, length, x_parts, wq, wk, wv, wg, pages):
-    shards, rows, width = x_parts.shape
+def attend(found, length, shards, queries, global_rows, key_rows, value_rows, pages):
+    rows, width = key_rows.shape
     longest = found.shape[0] * PAGE
     return pl.pallas_call(
         attention_kernel,
-        out_shape=jax.ShapeDtypeStruct(x_parts.shape, BF16),
-        in_specs=[SMEM, SMEM, VMEM, VMEM, VMEM, VMEM, VMEM, ANY],
+        out_shape=jax.ShapeDtypeStruct((shards, rows, width), BF16),
+        in_specs=[SMEM, SMEM] + [VMEM] * 4 + [ANY],
         out_specs=VMEM,
         scratch_shapes=[
-            pltpu.VMEM((rows, shards * width), BF16),
             pltpu.VMEM((longest, width), BF16),
             pltpu.VMEM((longest, width), BF16),
             pltpu.VMEM((longest // KEY_BLOCK, 2 * rows, KEY_BLOCK), F32),
@@ -287,7 +362,7 @@
         ],
         compiler_params=pltpu.CompilerParams(vmem_limit_bytes=56 << 20),
         name="attention",
-    )(found, length, x_parts, wq, wk, wv, wg, pages)
+    )(found, length, queries, global_rows, key_rows, value_rows, pages)
 
 
 def normalize(total, gain, bias, width):
@@ -298,7 +373,7 @@
 
 
 def ffn_kernel(
-    att, x_ref, accept, w_out, up_a, up_b, down_a, down_b, g1, b1, g2, b2, out, wide, hidden, acc
+    column, att, x_ref, accept, w_out, up_a, up_b, down_a, down_b, g1, b1, g2, b2, out, wide, hidden, acc
 ):
     step = pl.program_id(0)
     shards, rows, width = x_ref.shape
@@ -333,11 +408,18 @@
     def _():
         result = normalize(acc[...], g2[...], b2[...], full)
         chosen = accept[...] != 0
-        for i in range(shards):
-            out[i] = jnp.where(chosen, result[:, i * width : (i + 1) * width], x_ref[i])
-
-
-def feed_forward(att, x_parts, accept, w_out, up, down, g1, b1, g2, b2):
+        if out.shape[0] == shards:
+            for i in range(shards):
+                out[i] = jnp.where(chosen, result[:, i * width : (i + 1) * width], x_ref[i])
+        else:
+            for i in range(shards):
+
+                @pl.when(column[0] == i)
+                def _():
+                    out[0] = jnp.where(chosen, result[:, i * width : (i + 1) * width], x_ref[i])
+
+
+def feed_forward(column, outs, att, x_parts, accept, w_out, up, down, g1, b1, g2, b2):
     shards, rows, width = x_parts.shape
     full = shards * width
 
@@ -350,8 +432,9 @@
     return pl.pallas_call(
         ffn_kernel,
         grid=(up[0].shape[0] // PER,),
-        out_shape=jax.ShapeDtypeStruct(x_parts.shape, BF16),
+        out_shape=jax.ShapeDtypeStruct((outs, rows, width), BF16),
         in_specs=[
+            SMEM,
             fixed(x_parts.shape),
             fixed(x_parts.shape),
             fixed((rows, 1)),
@@ -362,7 +445,7 @@
             part(down[1]),
         ]
         + [fixed((1, full))] * 4,
-        out_specs=pl.BlockSpec(x_parts.shape, lambda i: (0, 0, 0)),
+        out_specs=pl.BlockSpec((outs, rows, width), lambda i: (0, 0, 0)),
         scratch_shapes=[
             pltpu.VMEM((rows, full), BF16),
             pltpu.VMEM((rows, full), BF16),
@@ -372,7 +455,7 @@
             dimension_semantics=("arbitrary",), vmem_limit_bytes=60 << 20
         ),
         name="feed_forward",
-    )(att, x_parts, accept, w_out, up[0], up[1], down[0], down[1], g1, b1, g2, b2)
+    )(column, att, x_parts, accept, w_out, up[0], up[1], down[0], down[1], g1, b1, g2, b2)
 
 
 def to_all(copies):
@@ -406,7 +489,9 @@
     me = lax.axis_index("pages")
     shard = lax.axis_index("mlp")
     rows, width = embeddings.shape
-    pages, found, x_parts = pages_to_owners(page_table, cache_keys, cache_values, embeddings)
+    pages, found, x_parts, (w_up, w_down, w_out) = pages_to_owners(
+        page_table, cache_keys, cache_values, (embeddings, w_up, w_down, w_out)
+    )
     length = lax.dynamic_slice_in_dim(lengths, me, 1, 0)
 
     core = me % 2
@@ -420,11 +505,13 @@
     down_other = lax.ppermute(down_mine, "pages", core_pair())
     norms = [v.reshape(1, -1) for v in (norm1_gain, norm1_bias, norm2_gain, norm2_bias)]
 
+    column = shard.reshape(1).astype(jnp.int32)
     for pass_index in range(2):
-        attention = attend(
-            found, length, x_parts, w_query, w_key, w_value, w_global_query, pages
-        )
+        projected = project_all(x_parts, w_query, w_key, w_value, w_global_query)
+        attention = attend(found, length, shards, *projected, pages)
         x_parts = feed_forward(
+            column,
+            shards if pass_index == 0 else 1,
             to_all(attention),
             x_parts,
             accept[pass_index].reshape(rows, 1),
@@ -433,7 +520,7 @@
             (down_mine, down_other),
             *norms,
         )
-    return lax.dynamic_index_in_dim(x_parts, shard, 0, keepdims=False)
+    return x_parts.reshape(rows, width)
 
 
 def solution(mesh):

time: 250 us -> 250 us (level)
  Pallas kernels: 56 us -> 60.4 us
  local copies, waits for them, and re-layouts: 9.83 us -> 6.32 us
    all_gather x1, waiting for transfers between devices: 0.01 us -> 17.1 us  [per_device(): w_out_all = lax.all_gather(w_out, 'mlp', axis=0, tiled=True)]
    all_to_all x2, waiting for transfers between devices: 42.5 us -> 25.4 us  [exchange(): lax.all_to_all(pages.reshape((holders, shape[0] // holders) + shape[1:]),...]
    all_to_all x2, waiting for transfers between devices: 33.8 us -> 19.3 us  [to_all(): return lax.all_to_all(copies, 'mlp', 0, 0, tiled=True)]
    all_gather x1, waiting for transfers between devices: 30.7 us -> 43 us  [per_device(): down_mine = lax.all_gather(down_half, 'mlp', axis=0)]
    pallas_call x4 -> x6, Pallas kernels: 31.9 us -> 36.5 us  [the longest x2 19.1 us: attend(): pl.pallas_call(attention_kernel, out_shape=jax.ShapeDtypeStruct((shards,...]
  transfers between devices with their start and end apart: 9 -> 9, of which waited for: 5 -> 6; matrix products, arithmetic and copies ran while one was open for 5% -> 3% of each run, Pallas kernels for 9% -> 7%
where the time goes in v1:
time: 250 us; the launch traced here: 248 us
  waiting for transfers between devices  105 us (42%)
  Pallas kernels  60.4 us (24%)
  starting transfers between devices  29.3 us (12%)
  blocking collectives  28.4 us (11%)
  between operations  14.1 us (6%)
  local copies, waits for them, and re-layouts  6.32 us (3%)
  other arithmetic  4.88 us (2%)
    all_gather x1, waiting for transfers between devices, per_device(): down_mine = lax.all_gather(down_half, 'mlp', axis=0)  43 us
    all_gather x1, blocking collectives, pages_to_owners(): x_parts = lax.all_gather(later[0], 'mlp', axis=0)  28.4 us
    all_to_all x2, waiting for transfers between devices, exchange(): lax.all_to_all(pages.reshape((holders, shape[0] // holders) + shape[1:]),...  25.4 us
    pallas_call x2, Pallas kernels, feed_forward(): pl.pallas_call(ffn_kernel, grid=(up[0].shape[0] // PER,), out_shape=jax.S...  23.9 us
    all_to_all x2, waiting for transfers between devices, to_all(): return lax.all_to_all(copies, 'mlp', 0, 0, tiled=True)  19.3 us
    pallas_call x2, Pallas kernels, attend(): pl.pallas_call(attention_kernel, out_shape=jax.ShapeDtypeStruct((shards,...  19.1 us
    all_gather x1, waiting for transfers between devices, per_device(): w_out_all = lax.all_gather(w_out, 'mlp', axis=0, tiled=True)  17.1 us
    all_to_all x2, starting transfers between devices, exchange(): lax.all_to_all(pages.reshape((holders, shape[0] // holders) + shape[1:]),...  16.4 us
  transfers between devices with their start and end apart: 9, of which 6 were waited for; matrix products, arithmetic and copies ran while one was open for 3% of the time, Pallas kernels for 7%

profile of v1, /device:TPU:9, one launch (start us, length us, event | category | flops | bytes accessed | tf_op | source)
XLA Modules:
  0.0 248.3 jit_solution(11458126608497236206)
XLA Ops:
  6.5 0.0 copy-start
  6.5 0.0 all-gather.9.cloned.1.call-start
  6.5 0.6 pad_add_fusion.1.where_and_turn
  7.2 6.4 %pack_pages.7 = bf16[64,2,128,128]{3,2,1,0:T(8,128)(2,1)} custom-call(s32[2]{0:T(128)} %pad_add_fusion.1.where_and_turn, s32[32,64]{1,0:T(8,128)} %page_table.1, bf16[64,128,128]{2,1,0:T(8,128)(2,1)} %keys.1, bf16[64,128,128]{2,1,0:T(8,128)(2,1)} %values.1), custom_call_target="tpu_custom_call" | custom-call | tf_op jit(solution)/shard_map/pack_pages/pallas_call | solution.py:166
  13.7 0.0 copy-done
  13.7 0.9 constant_dynamic-slice_fusion.1
  14.5 0.0 all-gather.9.cloned.1.call-update
  14.6 0.0 copy-start.5
  14.6 0.0 copy-start.4
  14.6 0.0 copy-start.6
  14.6 9.7 %all-to-all-start.1 = ((bf16[32,2,2,128,128]{4,3,2,1,0:T(8,128)(2,1)}), bf16[32,2,2,128,128]{4,3,2,1,0:T(8,128)(2,1)}, u32[]{:S(2)}, u32[]{:S(2)}) async-start(bf16[32,2,2,128,128]{4,3,2,1,0:T(8,128)(2,1)} %bitcast.72), calls=%async_computation.1 | async-start | bytes 8388608 | tf_op jit(solution)/shard_map/all_to_all | solution.py:198
  24.3 0.0 all-gather.11.cloned.1.call-start
  24.3 0.0 copy-done.5
  24.3 0.9 constant_dynamic-slice_fusion
  25.2 0.0 all-gather.11.cloned.1.call-update
  25.2 0.0 copy-done.4
  25.3 1.2 convert_reduce_fusion.2
  26.4 0.8 convert_reduce_fusion.3
  27.2 0.3 convert_reduce_fusion
  27.6 0.7 reduce_max.9
  29.0 0.2 convert_reduce_fusion.1
  29.2 0.1 select_reduce_fusion.2
  29.4 0.1 copy.23
  29.5 0.6 sub.64.table
  30.1 0.0 copy-done.6
  30.1 28.4 %all-gather = bf16[2048,128]{1,0:T(8,128)(2,1)} all-gather(bf16[256,128]{1,0:T(8,128)(2,1)S(1)} %copy-done.6), channel_id=2, replica_groups=mesh['pages'=32,'mlp'=8] {'mlp'}, dimensions={0}, use_global_device_ids=true | all-gather | bytes 589824 | tf_op jit(solution)/shard_map/all_gather | solution.py:211
  58.5 19.8 %all-to-all-done.1 = bf16[32,2,2,128,128]{4,3,2,1,0:T(8,128)(2,1)} async-done(((bf16[32,2,2,128,128]{4,3,2,1,0:T(8,128)(2,1)}), bf16[32,2,2,128,128]{4,3,2,1,0:T(8,128)(2,1)}, u32[]{:S(2)}, u32[]{:S(2)}) %all-to-all-start.1) | async-done | bytes 4194336 | tf_op jit(solution)/shard_map/all_to_all | solution.py:198
  78.3 0.0 copy-start.1
  78.3 5.6 %repack_pages.7 = bf16[64,2,128,128]{3,2,1,0:T(8,128)(2,1)} custom-call(s32[64]{0:T(128)} %sub.64.table, bf16[64,2,128,128]{3,2,1,0:T(8,128)(2,1)} %bitcast.5.got), custom_call_target="tpu_custom_call" | custom-call | tf_op jit(solution)/shard_map/repack_pages/pallas_call | solution.py:184
  83.9 0.0 copy-done.1
  83.9 0.0 copy-start.9
  83.9 6.8 %all-to-all-start.2 = ((bf16[32,2,2,128,128]{4,3,2,1,0:T(8,128)(2,1)}), bf16[32,2,2,128,128]{4,3,2,1,0:T(8,128)(2,1)}, u32[]{:S(2)}, u32[]{:S(2)}) async-start(bf16[32,2,2,128,128]{4,3,2,1,0:T(8,128)(2,1)} %bitcast.65), calls=%async_computation.2 | async-start | bytes 8388608 | tf_op jit(solution)/shard_map/all_to_all | solution.py:198
  90.7 0.0 copy-start.8
  90.7 0.0 all-gather.7.cloned.1.call-start
  90.7 0.0 all-gather.9.cloned.1.call-done
  90.8 0.4 collective-permute-start
  91.2 43.0 %all-gather.11.cloned.1.call-done = bf16[2048,1024]{1,0:T(8,128)(2,1)} async-done(((bf16[256,1024]{1,0:T(8,128)(2,1)}), bf16[2048,1024]{1,0:T(8,128)(2,1)}) %all-gather.11.cloned.1.call-update) | async-done | bytes 4194320 | tf_op jit(solution)/shard_map/all_gather | solution.py:503
  134.2 0.7 collective-permute-start.1
  134.9 0.0 all-gather.7.cloned.1.call-update
  134.9 0.0 copy-done.9
  134.9 0.6 dynamic_slice.17.length
  135.5 0.2 convert_reduce_fusion.4
  135.7 0.1 select_reduce_fusion.3
  135.8 0.6 compare_select_fusion.1.found
  136.4 2.7 %project.2 = (bf16[512,128]{1,0:T(8,128)(2,1)}, bf16[512,128]{1,0:T(8,128)(2,1)}, bf16[256,128]{1,0:T(8,128)(2,1)}, bf16[256,128]{1,0:T(8,128)(2,1)}) custom-call(bf16[8,256,128]{2,1,0:T(8,128)(2,1)} %bitcast.73, bf16[1024,128]{1,0:T(8,128)(2,1)} %wq.3, bf16[1024,128]{1,0:T(8,128)(2,1)} %wk.3, bf16[1024,128]{1,0:T(8,128)(2,1)} %wv.3, bf16[1024,128]{1,0:T(8,128)(2,1)} %wg.3), custom_call_target="tpu_custom_call" | custom-call | tf_op jit(solution)/shard_map/project/pallas_call | solution.py:251
  139.1 5.6 %all-to-all-done.2 = bf16[32,2,2,128,128]{4,3,2,1,0:T(8,128)(2,1)} async-done(((bf16[32,2,2,128,128]{4,3,2,1,0:T(8,128)(2,1)}), bf16[32,2,2,128,128]{4,3,2,1,0:T(8,128)(2,1)}, u32[]{:S(2)}, u32[]{:S(2)}) %all-to-all-start.2) | async-done | bytes 4194336 | tf_op jit(solution)/shard_map/all_to_all | solution.py:198
  144.7 9.6 %attention.2 = bf16[8,256,128]{2,1,0:T(8,128)(2,1)} custom-call(s32[64]{0:T(128)} %compare_select_fusion.1.found, s32[1]{0:T(128)} %dynamic_slice.17.length, bf16[512,128]{1,0:T(8,128)(2,1)} %get-tuple-element.306.queries, bf16[512,128]{1,0:T(8,128)(2,1)} %get-tuple-element.307.global_rows, bf16[256,128]{1,0:T(8,128)(2,1)} %get-tuple-element.308.key_rows, ...), custom_call_target="tpu_custom_call" | custom-call | tf_op jit(solution)/shard_map/attention/pallas_call | solution.py:349
  154.4 8.2 %all-to-all-start.3 = ((bf16[8,256,128]{2,1,0:T(8,128)(2,1)}), bf16[8,256,128]{2,1,0:T(8,128)(2,1)S(1)}, u32[]{:S(2)}, u32[]{:S(2)}) async-start(bf16[8,256,128]{2,1,0:T(8,128)(2,1)} %attention.2), calls=%async_computation.3 | async-start | bytes 1048576 | tf_op jit(solution)/shard_map/all_to_all | solution.py:462
  162.5 0.0 copy-done.8
  162.6 0.8 copy.24.accept
  163.4 17.1 %all-gather.7.cloned.1.call-done.w_out = bf16[1024,1024]{1,0:T(8,128)(2,1)} async-done(((bf16[128,1024]{1,0:T(8,128)(2,1)}), bf16[1024,1024]{1,0:T(8,128)(2,1)}) %all-gather.7.cloned.1.call-update) | async-done | bytes 2097168 | tf_op jit(solution)/shard_map/all_gather | solution.py:501
  180.5 3.5 %all-to-all-done.3.att = bf16[8,256,128]{2,1,0:T(8,128)(2,1)S(1)} async-done(((bf16[8,256,128]{2,1,0:T(8,128)(2,1)}), bf16[8,256,128]{2,1,0:T(8,128)(2,1)S(1)}, u32[]{:S(2)}, u32[]{:S(2)}) %all-to-all-start.3) | async-done | bytes 524320 | tf_op jit(solution)/shard_map/all_to_all | solution.py:462
  184.0 0.0 collective-permute-done.up_b
  184.0 0.0 collective-permute-done.1.down_b
  184.0 0.8 copy-done.2
  184.8 12.0 %feed_forward.2.x_ref = bf16[8,256,128]{2,1,0:T(8,128)(2,1)} custom-call(s32[1]{0:T(128)} %bitcast.column, bf16[8,256,128]{2,1,0:T(8,128)(2,1)} %copy-done.2, bf16[8,256,128]{2,1,0:T(8,128)(2,1)} %bitcast.74, s32[256,1]{1,0:T(8,128)} %copy.24.accept, bf16[1024,1024]{1,0:T(8,128)(2,1)} %all-gather.7.cloned.1.call-done.w_out, bf16[8,1024,256]{2,1,0:T(8,128)(2,1)} %bitcast.67, ...), custom_call_target="tpu_custom_call" | custom-call | tf_op jit(solution)/shard_map/feed_forward/pallas_call | solution.py:432
  196.8 2.7 %project.3 = (bf16[512,128]{1,0:T(8,128)(2,1)}, bf16[512,128]{1,0:T(8,128)(2,1)}, bf16[256,128]{1,0:T(8,128)(2,1)}, bf16[256,128]{1,0:T(8,128)(2,1)}) custom-call(bf16[8,256,128]{2,1,0:T(8,128)(2,1)} %feed_forward.2.x_ref, bf16[1024,128]{1,0:T(8,128)(2,1)} %wq.3, bf16[1024,128]{1,0:T(8,128)(2,1)} %wk.3, bf16[1024,128]{1,0:T(8,128)(2,1)} %wv.3, ...), custom_call_target="tpu_custom_call" | custom-call | tf_op jit(solution)/shard_map/project/pallas_call | solution.py:251
  199.5 9.5 %attention.3 = bf16[8,256,128]{2,1,0:T(8,128)(2,1)} custom-call(s32[64]{0:T(128)} %compare_select_fusion.1.found, s32[1]{0:T(128)} %dynamic_slice.17.length, bf16[512,128]{1,0:T(8,128)(2,1)} %get-tuple-element.315.queries, bf16[512,128]{1,0:T(8,128)(2,1)} %get-tuple-element.316.global_rows, bf16[256,128]{1,0:T(8,128)(2,1)} %get-tuple-element.317.key_rows, ...), custom_call_target="tpu_custom_call" | custom-call | tf_op jit(solution)/shard_map/attention/pallas_call | solution.py:349
  209.0 3.5 %all-to-all-start.4 = ((bf16[8,256,128]{2,1,0:T(8,128)(2,1)}), bf16[8,256,128]{2,1,0:T(8,128)(2,1)S(1)}, u32[]{:S(2)}, u32[]{:S(2)}) async-start(bf16[8,256,128]{2,1,0:T(8,128)(2,1)} %attention.3), calls=%async_computation.4 | async-start | bytes 1048576 | tf_op jit(solution)/shard_map/all_to_all | solution.py:462
  212.5 0.8 copy.25.accept
  213.3 15.8 %all-to-all-done.4.att = bf16[8,256,128]{2,1,0:T(8,128)(2,1)S(1)} async-done(((bf16[8,256,128]{2,1,0:T(8,128)(2,1)}), bf16[8,256,128]{2,1,0:T(8,128)(2,1)S(1)}, u32[]{:S(2)}, u32[]{:S(2)}) %all-to-all-start.4) | async-done | bytes 524320 | tf_op jit(solution)/shard_map/all_to_all | solution.py:462
  229.1 0.0 copy-start.3
  229.1 0.8 copy-done.3
  229.9 11.9 %feed_forward.3 = bf16[1,256,128]{2,1,0:T(8,128)(2,1)} custom-call(s32[1]{0:T(128)} %bitcast.column, bf16[8,256,128]{2,1,0:T(8,128)(2,1)} %copy-done.3, bf16[8,256,128]{2,1,0:T(8,128)(2,1)} %feed_forward.2.x_ref, s32[256,1]{1,0:T(8,128)} %copy.25.accept, bf16[1024,1024]{1,0:T(8,128)(2,1)} %all-gather.7.cloned.1.call-done.w_out, ...), custom_call_target="tpu_custom_call" | custom-call | tf_op jit(solution)/shard_map/feed_forward/pallas_call | solution.py:432
  (13 shorter events, 0.1 us)
Async XLA Ops:
  6.5 7.1 %copy-start = (bf16[1024,512]{1,0:T(8,128)(2,1)S(1)}, bf16[1024,512]{1,0:T(8,128)(2,1)}, u32[]{:S(2)}) copy-start(bf16[1024,512]{1,0:T(8,128)(2,1)} %param.25) | copy-start | bytes 3145732
  6.5 84.2 %all-gather.9.cloned.1.call-start = ((), (), s32[]{:S(2)}) async-start(), calls=%async_computation.6 | async-start | bytes 4718592 | tf_op jit(solution)/shard_map/all_gather | solution.py:502
  14.6 9.8 %copy-start.5 = (bf16[512,1024]{1,0:T(8,128)(2,1)S(1)}, bf16[512,1024]{1,0:T(8,128)(2,1)}, u32[]{:S(2)}) copy-start(bf16[512,1024]{1,0:T(8,128)(2,1)} %param.26) | copy-start | bytes 3145732
  14.6 10.7 %copy-start.4 = (s32[32,64]{1,0:T(8,128)S(1)}, s32[32,64]{1,0:T(8,128)}, u32[]{:S(2)}) copy-start(s32[32,64]{1,0:T(8,128)} %page_table.1) | copy-start | bytes 24580
  14.6 15.5 %copy-start.6 = (bf16[256,128]{1,0:T(8,128)(2,1)S(1)}, bf16[256,128]{1,0:T(8,128)(2,1)}, u32[]{:S(2)}) copy-start(bf16[256,128]{1,0:T(8,128)(2,1)} %param.19) | copy-start | bytes 196612
  14.6 63.7 %all-to-all-start.1 = ((bf16[32,2,2,128,128]{4,3,2,1,0:T(8,128)(2,1)}), bf16[32,2,2,128,128]{4,3,2,1,0:T(8,128)(2,1)}, u32[]{:S(2)}, u32[]{:S(2)}) async-start(bf16[32,2,2,128,128]{4,3,2,1,0:T(8,128)(2,1)} %bitcast.72), calls=%async_computation.1 | async-start | bytes 8388608 | tf_op jit(solution)/shard_map/all_to_all | solution.py:198
  24.3 109.9 %all-gather.11.cloned.1.call-start = ((), (), s32[]{:S(2)}) async-start(), calls=%async_computation.7 | async-start | bytes 4718592 | tf_op jit(solution)/shard_map/all_gather | solution.py:503
  78.3 5.6 %copy-start.1 = (bf16[64,128,128]{2,1,0:T(8,128)(2,1)S(1)}, bf16[64,128,128]{2,1,0:T(8,128)(2,1)}, u32[]{:S(2)}) copy-start(bf16[64,128,128]{2,1,0:T(8,128)(2,1)} %keys.1) | copy-start | bytes 6291460
  83.9 51.0 %copy-start.9 = (s32[32]{0:T(128)S(1)}, s32[32]{0:T(128)}, u32[]{:S(2)}) copy-start(s32[32]{0:T(128)} %param.33) | copy-start | bytes 388
  83.9 60.8 %all-to-all-start.2 = ((bf16[32,2,2,128,128]{4,3,2,1,0:T(8,128)(2,1)}), bf16[32,2,2,128,128]{4,3,2,1,0:T(8,128)(2,1)}, u32[]{:S(2)}, u32[]{:S(2)}) async-start(bf16[32,2,2,128,128]{4,3,2,1,0:T(8,128)(2,1)} %bitcast.65), calls=%async_computation.2 | async-start | bytes 8388608 | tf_op jit(solution)/shard_map/all_to_all | solution.py:198
  90.7 71.9 %copy-start.8 = (s32[2,256]{1,0:T(2,128)S(1)}, s32[2,256]{1,0:T(2,128)}, u32[]{:S(2)}) copy-start(s32[2,256]{1,0:T(2,128)} %param.35) | copy-start | bytes 6148
  90.7 89.8 %all-gather.7.cloned.1.call-start = ((), (), s32[]{:S(2)}) async-start(), calls=%async_computation.5 | async-start | bytes 2359296 | tf_op jit(solution)/shard_map/all_gather | solution.py:501
  90.8 93.2 %collective-permute-start = (bf16[8,1024,256]{2,1,0:T(8,128)(2,1)}, bf16[8,1024,256]{2,1,0:T(8,128)(2,1)}, u32[]{:S(2)}, u32[]{:S(2)}) collective-permute-start(bf16[8,1024,256]{2,1,0:T(8,128)(2,1)} %bitcast.66), channel_id=1, source_target_pairs={{0,8},{8,0},{16,24},{24,16},{32,40},{40,32},{48,56},{56,48},{64,72... | collective-permute-start | bytes 12582920 | tf_op jit(solution)/shard_map/ppermute | solution.py:504
  134.2 49.8 %collective-permute-start.1 = (bf16[8,256,1024]{2,1,0:T(8,128)(2,1)}, bf16[8,256,1024]{2,1,0:T(8,128)(2,1)}, u32[]{:S(2)}, u32[]{:S(2)}) collective-permute-start(bf16[8,256,1024]{2,1,0:T(8,128)(2,1)} %bitcast.69), channel_id=1, source_target_pairs={{0,8},{8,0},{16,24},{24,16},{32,40},{40,32},{48,56},{56,48},{64,72... | collective-permute-start | bytes 12582920 | tf_op jit(solution)/shard_map/ppermute | solution.py:505
  154.4 29.7 %all-to-all-start.3 = ((bf16[8,256,128]{2,1,0:T(8,128)(2,1)}), bf16[8,256,128]{2,1,0:T(8,128)(2,1)S(1)}, u32[]{:S(2)}, u32[]{:S(2)}) async-start(bf16[8,256,128]{2,1,0:T(8,128)(2,1)} %attention.2), calls=%async_computation.3 | async-start | bytes 1048576 | tf_op jit(solution)/shard_map/all_to_all | solution.py:462
  184.0 0.8 copy-start.2
  209.0 20.1 %all-to-all-start.4 = ((bf16[8,256,128]{2,1,0:T(8,128)(2,1)}), bf16[8,256,128]{2,1,0:T(8,128)(2,1)S(1)}, u32[]{:S(2)}, u32[]{:S(2)}) async-start(bf16[8,256,128]{2,1,0:T(8,128)(2,1)} %attention.3), calls=%async_computation.4 | async-start | bytes 1048576 | tf_op jit(solution)/shard_map/all_to_all | solution.py:462
  229.1 0.8 copy-start.3
Sparse Core Ops, SparseCore 0:
  14.7 64.2 all-gather.8
  80.7 53.4 all-gather.10
  136.0 44.4 all-gather.6

commit v2 on v1

--- a/solution.py
+++ b/solution.py
@@ -258,23 +258,11 @@
     )(x_parts, wq, wk, wv, wg)
 
 
-def attention_kernel(
-    found,
-    length,
-    queries,
-    global_rows,
-    key_rows,
-    value_rows,
-    pages,
-    out,
-    key_buf,
-    value_buf,
-    kept,
-    peak,
-    acc,
-    ksem,
-    vsem,
-):
+def attention_kernel(inner, found, length, *refs):
+    given = refs[: 5 if inner else 4]
+    pages, out, key_buf, value_buf, kept, peak, acc, ksem, vsem = refs[len(given) :][:9]
+    projected = refs[len(given) + 9 :]
+    queries, global_rows, key_rows, value_rows = projected[:4] if inner else given
     per_block = KEY_BLOCK // PAGE
     shards, rows, width = out.shape
     limit = length[0]
@@ -292,6 +280,8 @@
 
     lax.fori_loop(0, blocks, functools.partial(fetch, part=0, buf=key_buf, sem=ksem), 0)
     lax.fori_loop(0, blocks, functools.partial(fetch, part=1, buf=value_buf, sem=vsem), 0)
+    if inner:
+        project_kernel(*given, *projected)
     def scores_of(left, keys):
         return lax.dot_general(
             left, keys, (((1,), (1,)), ((), ())), preferred_element_type=F32
@@ -343,26 +333,36 @@
         out[i] = result
 
 
-def attend(found, length, shards, queries, global_rows, key_rows, value_rows, pages):
-    rows, width = key_rows.shape
+def attend(found, length, shards, given, pages):
+    inner = len(given) == 5
+    rows, width = given[0].shape[1:] if inner else given[2].shape
     longest = found.shape[0] * PAGE
+    scratch = [
+        pltpu.VMEM((longest, width), BF16),
+        pltpu.VMEM((longest, width), BF16),
+        pltpu.VMEM((longest // KEY_BLOCK, 2 * rows, KEY_BLOCK), F32),
+        pltpu.VMEM((2 * rows, 128), F32),
+        pltpu.VMEM((2 * rows, 2 * width), F32),
+        pltpu.SemaphoreType.DMA((longest // KEY_BLOCK,)),
+        pltpu.SemaphoreType.DMA((longest // KEY_BLOCK,)),
+    ]
+    if inner:
+        scratch += [
+            pltpu.VMEM((2 * rows, width), BF16),
+            pltpu.VMEM((2 * rows, width), BF16),
+            pltpu.VMEM((rows, width), BF16),
+            pltpu.VMEM((rows, width), BF16),
+            pltpu.VMEM((rows, shards * width), BF16),
+        ]
     return pl.pallas_call(
-        attention_kernel,
+        functools.partial(attention_kernel, inner),
         out_shape=jax.ShapeDtypeStruct((shards, rows, width), BF16),
-        in_specs=[SMEM, SMEM] + [VMEM] * 4 + [ANY],
+        in_specs=[SMEM, SMEM] + [VMEM] * len(given) + [ANY],
         out_specs=VMEM,
-        scratch_shapes=[
-            pltpu.VMEM((longest, width), BF16),
-            pltpu.VMEM((longest, width), BF16),
-            pltpu.VMEM((longest // KEY_BLOCK, 2 * rows, KEY_BLOCK), F32),
-            pltpu.VMEM((2 * rows, 128), F32),
-            pltpu.VMEM((2 * rows, 2 * width), F32),
-            pltpu.SemaphoreType.DMA((longest // KEY_BLOCK,)),
-            pltpu.SemaphoreType.DMA((longest // KEY_BLOCK,)),
-        ],
+        scratch_shapes=scratch,
         compiler_params=pltpu.CompilerParams(vmem_limit_bytes=56 << 20),
         name="attention",
-    )(found, length, queries, global_rows, key_rows, value_rows, pages)
+    )(found, length, *given, pages)
 
 
 def normalize(total, gain, bias, width):
@@ -373,16 +373,43 @@
 
 
 def ffn_kernel(
-    column, att, x_ref, accept, w_out, up_a, up_b, down_a, down_b, g1, b1, g2, b2, out, wide, hidden, acc
+    place,
+    att,
+    x_ref,
+    accept,
+    low_a,
+    low_b,
+    up_a,
+    up_b,
+    down_a,
+    down_b,
+    g1,
+    b1,
+    g2,
+    b2,
+    out,
+    wide,
+    hidden,
+    acc,
+    w_out,
+    w_sem,
 ):
     step = pl.program_id(0)
     shards, rows, width = x_ref.shape
     full = shards * width
+    column, core = place[0], place[1]
 
     @pl.when(step == 0)
     def _():
+        half = width // 2
+        skip = down_a.shape[1]
+        for i in range(shards):
+            for low, owner in ((low_a, core), (low_b, 1 - core)):
+                at = pl.ds(pl.multiple_of(i * width + owner * half, half), half)
+                pltpu.make_async_copy(low.at[i, skip : skip + half], w_out.at[at], w_sem).start()
         for i in range(shards):
             wide[:, i * width : (i + 1) * width] = att[i]
+        pltpu.make_async_copy(w_out, w_out, w_sem).wait()
         total = jnp.dot(wide[...], w_out[...], preferred_element_type=F32)
         for i in range(shards):
             wide[:, i * width : (i + 1) * width] = x_ref[i]
@@ -414,48 +441,43 @@
         else:
             for i in range(shards):
 
-                @pl.when(column[0] == i)
+                @pl.when(column == i)
                 def _():
                     out[0] = jnp.where(chosen, result[:, i * width : (i + 1) * width], x_ref[i])
 
 
-def feed_forward(column, outs, att, x_parts, accept, w_out, up, down, g1, b1, g2, b2):
+def feed_forward(place, outs, att, x_parts, accept, up, low, g1, b1, g2, b2):
     shards, rows, width = x_parts.shape
     full = shards * width
+    units = up[0].shape[2]
 
     def fixed(shape):
         return pl.BlockSpec(shape, lambda i: (0,) * len(shape), pipeline_mode=pl.Buffered(1))
 
-    def part(array):
-        return pl.BlockSpec((PER,) + array.shape[1:], lambda i: (i, 0, 0))
+    def part(*shape):
+        return pl.BlockSpec((PER,) + shape, lambda i: (i, 0, 0))
 
     return pl.pallas_call(
         ffn_kernel,
-        grid=(up[0].shape[0] // PER,),
+        grid=(shards // PER,),
         out_shape=jax.ShapeDtypeStruct((outs, rows, width), BF16),
-        in_specs=[
-            SMEM,
-            fixed(x_parts.shape),
-            fixed(x_parts.shape),
-            fixed((rows, 1)),
-            fixed(w_out.shape),
-            part(up[0]),
-            part(up[1]),
-            part(down[0]),
-            part(down[1]),
-        ]
+        in_specs=[SMEM, fixed(x_parts.shape), fixed(x_parts.shape), fixed((rows, 1)), ANY, ANY]
+        + [part(full, units)] * 2
+        + [part(units, full)] * 2
         + [fixed((1, full))] * 4,
         out_specs=pl.BlockSpec((outs, rows, width), lambda i: (0, 0, 0)),
         scratch_shapes=[
             pltpu.VMEM((rows, full), BF16),
             pltpu.VMEM((rows, full), BF16),
             pltpu.VMEM((rows, full), F32),
+            pltpu.VMEM((full, full), BF16),
+            pltpu.SemaphoreType.DMA,
         ],
         compiler_params=pltpu.CompilerParams(
             dimension_semantics=("arbitrary",), vmem_limit_bytes=60 << 20
         ),
         name="feed_forward",
-    )(column, att, x_parts, accept, w_out, up[0], up[1], down[0], down[1], g1, b1, g2, b2)
+    )(place, att, x_parts, accept, *low, *up, *low, g1, b1, g2, b2)
 
 
 def to_all(copies):
@@ -496,31 +518,28 @@
 
     core = me % 2
     half = w_up.shape[1] // 2
+    half_out = w_out.shape[0] // 2
     up_half = lax.dynamic_slice_in_dim(w_up, core * half, half, 1)
     down_half = lax.dynamic_slice_in_dim(w_down, core * half, half, 0)
-    w_out_all = lax.all_gather(w_out, "mlp", axis=0, tiled=True)
+    out_half = lax.dynamic_slice_in_dim(w_out, core * half_out, half_out, 0)
     up_mine = lax.all_gather(up_half, "mlp", axis=0)
-    down_mine = lax.all_gather(down_half, "mlp", axis=0)
-    up_other = lax.ppermute(up_mine, "pages", core_pair())
-    down_other = lax.ppermute(down_mine, "pages", core_pair())
+    low_mine = lax.all_gather(jnp.concatenate([down_half, out_half]), "mlp", axis=0)
     norms = [v.reshape(1, -1) for v in (norm1_gain, norm1_bias, norm2_gain, norm2_bias)]
-
-    column = shard.reshape(1).astype(jnp.int32)
-    for pass_index in range(2):
-        projected = project_all(x_parts, w_query, w_key, w_value, w_global_query)
-        attention = attend(found, length, shards, *projected, pages)
-        x_parts = feed_forward(
-            column,
-            shards if pass_index == 0 else 1,
-            to_all(attention),
-            x_parts,
-            accept[pass_index].reshape(rows, 1),
-            w_out_all,
-            (up_mine, up_other),
-            (down_mine, down_other),
-            *norms,
+    place = jnp.stack([shard, core]).astype(jnp.int32)
+    projections = (w_query, w_key, w_value, w_global_query)
+
+    def layer(outs, attention, x_parts, taken, up, low):
+        return feed_forward(
+            place, outs, to_all(attention), x_parts, taken.reshape(rows, 1), up, low, *norms
         )
-    return x_parts.reshape(rows, width)
+
+    attention = attend(found, length, shards, project_all(x_parts, *projections), pages)
+    attention, low_mine = lax.optimization_barrier((attention, low_mine))
+    up = (up_mine, lax.ppermute(up_mine, "pages", core_pair()))
+    low = (low_mine, lax.ppermute(low_mine, "pages", core_pair()))
+    middle = layer(shards, attention, x_parts, accept[0], up, low)
+    attention = attend(found, length, shards, (middle,) + projections, pages)
+    return layer(1, attention, middle, accept[1], up, low).reshape(rows, width)
 
 
 def solution(mesh):

time: 250 us -> 247 us (0.988); the launches traced: 248 us -> 243 us
  Pallas kernels: 60.4 us -> 56.6 us
    all_gather x2 -> x1, waiting for transfers between devices: 60.1 us -> 0.02 us  [per_device(): lax.all_gather(jnp.concatenate([down_half, out_half]), 'mlp', axis=0)]
    all_to_all x2, waiting for transfers between devices: 25.4 us -> 69.4 us  [exchange(): lax.all_to_all(pages.reshape((holders, shape[0] // holders) + shape[1:]),...]
    all_to_all x2, waiting for transfers between devices: 19.3 us -> 33.8 us  [to_all(): return lax.all_to_all(copies, 'mlp', 0, 0, tiled=True)]
    pallas_call x2 -> x1, Pallas kernels: 5.36 us -> 2.69 us  [project_all(): pl.pallas_call(project_kernel, out_shape=(doubled, doubled, single, singl...]
  transfers between devices with their start and end apart: 9 -> 8, of which waited for: 6 -> 4; matrix products, arithmetic and copies ran while one was open for 3% -> 4% of each run, Pallas kernels for 7% -> 6%
where the time goes in v2:
time: 247 us; the launch traced here: 243 us
  waiting for transfers between devices  103 us (42%)
  Pallas kernels  56.6 us (23%)
  blocking collectives  28.6 us (12%)
  starting transfers between devices  28 us (11%)
  between operations  14.4 us (6%)
  other arithmetic  6.26 us (3%)
  local copies, waits for them, and re-layouts  5.61 us (2%)
    all_to_all x2, waiting for transfers between devices, exchange(): lax.all_to_all(pages.reshape((holders, shape[0] // holders) + shape[1:]),...  69.4 us
    all_to_all x2, waiting for transfers between devices, to_all(): return lax.all_to_all(copies, 'mlp', 0, 0, tiled=True)  33.8 us
    all_gather x1, blocking collectives, pages_to_owners(): x_parts = lax.all_gather(later[0], 'mlp', axis=0)  28.6 us
    pallas_call x2, Pallas kernels, feed_forward(): pl.pallas_call(ffn_kernel, grid=(shards // PER,), out_shape=jax.ShapeDtyp...  26.2 us
    all_to_all x2, starting transfers between devices, exchange(): lax.all_to_all(pages.reshape((holders, shape[0] // holders) + shape[1:]),...  15.4 us
    pallas_call x2, Pallas kernels, attend(): pl.pallas_call(functools.partial(attention_kernel, inner), out_shape=jax....  15.4 us
    all_to_all x2, starting transfers between devices, to_all(): return lax.all_to_all(copies, 'mlp', 0, 0, tiled=True)  11.7 us
    pallas_call x1, Pallas kernels, pack_pages(): pl.pallas_call(pack_kernel, out_shape=jax.ShapeDtypeStruct(shape, BF16),...  6.87 us
  transfers between devices with their start and end apart: 8, of which 4 were waited for; matrix products, arithmetic and copies ran while one was open for 4% of the time, Pallas kernels for 6%

profile of v2, /device:TPU:9, one launch (start us, length us, event | category | flops | bytes accessed | tf_op | source)
XLA Modules:
  0.0 242.7 jit_solution(10411496677120208173)
XLA Ops:
  6.5 0.0 copy-start
  6.5 0.0 all-gather.6.cloned.1.call-start
  6.5 0.7 pad_add_fusion.2.where_and_turn
  7.2 0.0 copy-start.7
  7.2 6.9 %pack_pages.7 = bf16[64,2,128,128]{3,2,1,0:T(8,128)(2,1)} custom-call(s32[2]{0:T(128)} %pad_add_fusion.2.where_and_turn, s32[32,64]{1,0:T(8,128)} %page_table.1, bf16[64,128,128]{2,1,0:T(8,128)(2,1)} %keys.1, bf16[64,128,128]{2,1,0:T(8,128)(2,1)} %values.1), custom_call_target="tpu_custom_call" | custom-call | tf_op jit(solution)/shard_map/pack_pages/pallas_call | solution.py:166
  14.1 0.0 copy-done
  14.2 0.0 copy-done.7
  14.2 0.9 pad_maximum_fusion
  15.1 0.0 all-gather.6.cloned.1.call-update
  15.1 0.0 copy-start.5
  15.1 0.0 copy-start.4
  15.1 0.0 copy-start.6
  15.2 8.7 %all-to-all-start.1 = ((bf16[32,2,2,128,128]{4,3,2,1,0:T(8,128)(2,1)}), bf16[32,2,2,128,128]{4,3,2,1,0:T(8,128)(2,1)}, u32[]{:S(2)}, u32[]{:S(2)}) async-start(bf16[32,2,2,128,128]{4,3,2,1,0:T(8,128)(2,1)} %bitcast.72), calls=%async_computation.1 | async-start | bytes 8388608 | tf_op jit(solution)/shard_map/all_to_all | solution.py:198
  23.9 0.0 all-gather.8.cloned.1.call-start
  23.9 0.0 copy-done.5
  23.9 0.9 constant_dynamic-slice_fusion
  24.8 0.0 all-gather.8.cloned.1.call-update
  24.8 0.0 copy-done.4
  24.8 1.2 convert_reduce_fusion.2
  26.0 0.8 convert_reduce_fusion.3
  26.8 0.3 convert_reduce_fusion
  27.1 0.7 reduce_max.9
  28.5 0.2 convert_reduce_fusion.1
  28.8 0.1 select_reduce_fusion.2
  28.9 0.1 copy.23
  29.0 0.7 sub.64.table
  29.7 0.0 copy-done.6
  29.7 28.6 %all-gather = bf16[2048,128]{1,0:T(8,128)(2,1)} all-gather(bf16[256,128]{1,0:T(8,128)(2,1)S(1)} %copy-done.6), channel_id=2, replica_groups=mesh['pages'=32,'mlp'=8] {'mlp'}, dimensions={0}, use_global_device_ids=true | all-gather | bytes 589824 | tf_op jit(solution)/shard_map/all_gather | solution.py:211
  58.3 19.5 %all-to-all-done.1 = bf16[32,2,2,128,128]{4,3,2,1,0:T(8,128)(2,1)} async-done(((bf16[32,2,2,128,128]{4,3,2,1,0:T(8,128)(2,1)}), bf16[32,2,2,128,128]{4,3,2,1,0:T(8,128)(2,1)}, u32[]{:S(2)}, u32[]{:S(2)}) %all-to-all-start.1) | async-done | bytes 4194336 | tf_op jit(solution)/shard_map/all_to_all | solution.py:198
  77.9 0.0 copy-start.1
  77.9 5.4 %repack_pages.7 = bf16[64,2,128,128]{3,2,1,0:T(8,128)(2,1)} custom-call(s32[64]{0:T(128)} %sub.64.table, bf16[64,2,128,128]{3,2,1,0:T(8,128)(2,1)} %bitcast.6.got), custom_call_target="tpu_custom_call" | custom-call | tf_op jit(solution)/shard_map/repack_pages/pallas_call | solution.py:184
  83.3 0.0 copy-done.1
  83.3 0.0 copy-start.10
  83.3 6.8 %all-to-all-start.2 = ((bf16[32,2,2,128,128]{4,3,2,1,0:T(8,128)(2,1)}), bf16[32,2,2,128,128]{4,3,2,1,0:T(8,128)(2,1)}, u32[]{:S(2)}, u32[]{:S(2)}) async-start(bf16[32,2,2,128,128]{4,3,2,1,0:T(8,128)(2,1)} %bitcast.66), calls=%async_computation.2 | async-start | bytes 8388608 | tf_op jit(solution)/shard_map/all_to_all | solution.py:198
  90.1 0.0 copy-start.9
  90.1 0.0 copy-done.10
  90.1 0.7 dynamic_slice.20.length
  90.8 0.2 convert_reduce_fusion.4
  91.0 0.1 select_reduce_fusion.3
  91.0 0.5 compare_select_fusion.1.found
  91.6 2.7 %project.1 = (bf16[512,128]{1,0:T(8,128)(2,1)}, bf16[512,128]{1,0:T(8,128)(2,1)}, bf16[256,128]{1,0:T(8,128)(2,1)}, bf16[256,128]{1,0:T(8,128)(2,1)}) custom-call(bf16[8,256,128]{2,1,0:T(8,128)(2,1)} %bitcast.76, bf16[1024,128]{1,0:T(8,128)(2,1)} %refs_1_.1, bf16[1024,128]{1,0:T(8,128)(2,1)} %refs_2_.1, bf16[1024,128]{1,0:T(8,128)(2,1)} %refs_3_.1, ...), custom_call_target="tpu_custom_call" | custom-call | tf_op jit(solution)/shard_map/project/pallas_call | solution.py:251
  94.3 49.8 %all-to-all-done.2 = bf16[32,2,2,128,128]{4,3,2,1,0:T(8,128)(2,1)} async-done(((bf16[32,2,2,128,128]{4,3,2,1,0:T(8,128)(2,1)}), bf16[32,2,2,128,128]{4,3,2,1,0:T(8,128)(2,1)}, u32[]{:S(2)}, u32[]{:S(2)}) %all-to-all-start.2) | async-done | bytes 4194336 | tf_op jit(solution)/shard_map/all_to_all | solution.py:198
  144.1 7.5 %attention.2 = bf16[8,256,128]{2,1,0:T(8,128)(2,1)} custom-call(s32[64]{0:T(128)} %compare_select_fusion.1.found, s32[1]{0:T(128)} %dynamic_slice.20.length, bf16[512,128]{1,0:T(8,128)(2,1)} %get-tuple-element.304.refs_0_, bf16[512,128]{1,0:T(8,128)(2,1)} %get-tuple-element.305.refs_1_, bf16[256,128]{1,0:T(8,128)(2,1)} %get-tuple-element.306.refs_2_, ...), custom_call_target="tpu_custom_call" | custom-call | tf_op jit(solution)/shard_map/attention/pallas_call | solution.py:357
  151.6 0.0 all-gather.6.cloned.1.call-done
  151.7 0.4 collective-permute-start
  152.1 0.0 all-gather.8.cloned.1.call-done
  152.1 0.3 collective-permute-start.1
  152.5 8.2 %all-to-all-start.3 = ((bf16[8,256,128]{2,1,0:T(8,128)(2,1)}), bf16[8,256,128]{2,1,0:T(8,128)(2,1)S(1)}, u32[]{:S(2)}, u32[]{:S(2)}) async-start(bf16[8,256,128]{2,1,0:T(8,128)(2,1)} %attention.2), calls=%async_computation.3 | async-start | bytes 1048576 | tf_op jit(solution)/shard_map/all_to_all | solution.py:484
  160.6 0.0 copy-done.9
  160.7 0.8 copy.24.accept
  161.5 0.6 pad_add_fusion.1.place
  162.0 16.6 %all-to-all-done.3.att = bf16[8,256,128]{2,1,0:T(8,128)(2,1)S(1)} async-done(((bf16[8,256,128]{2,1,0:T(8,128)(2,1)}), bf16[8,256,128]{2,1,0:T(8,128)(2,1)S(1)}, u32[]{:S(2)}, u32[]{:S(2)}) %all-to-all-start.3) | async-done | bytes 524320 | tf_op jit(solution)/shard_map/all_to_all | solution.py:484
  178.6 0.0 copy-start.2
  178.6 0.0 collective-permute-done.1.up_b
  178.6 0.0 collective-permute-done.low_b.down_b
  178.6 0.8 copy-done.2
  179.4 13.2 %feed_forward.2.refs_0_.x_ref = bf16[8,256,128]{2,1,0:T(8,128)(2,1)} custom-call(s32[2]{0:T(128)} %pad_add_fusion.1.place, bf16[8,256,128]{2,1,0:T(8,128)(2,1)} %copy-done.2, bf16[8,256,128]{2,1,0:T(8,128)(2,1)} %bitcast.77, s32[256,1]{1,0:T(8,128)} %copy.24.accept, bf16[8,320,1024]{2,1,0:T(8,128)(2,1)} %bitcast.68, ...), custom_call_target="tpu_custom_call" | custom-call | tf_op jit(solution)/shard_map/feed_forward/pallas_call | solution.py:460
  192.6 7.9 %attention.3 = bf16[8,256,128]{2,1,0:T(8,128)(2,1)} custom-call(s32[64]{0:T(128)} %compare_select_fusion.1.found, s32[1]{0:T(128)} %dynamic_slice.20.length, bf16[8,256,128]{2,1,0:T(8,128)(2,1)} %feed_forward.2.refs_0_.x_ref, bf16[1024,128]{1,0:T(8,128)(2,1)} %refs_1_.1, bf16[1024,128]{1,0:T(8,128)(2,1)} %refs_2_.1, bf16[1024,128]{1,0:T(8,128)(2,1)} %refs_3_.1, ...), custom_call_target="tpu_custom_call" | custom-call | tf_op jit(solution)/shard_map/attention/pallas_call | solution.py:357
  200.5 3.5 %all-to-all-start.4 = ((bf16[8,256,128]{2,1,0:T(8,128)(2,1)}), bf16[8,256,128]{2,1,0:T(8,128)(2,1)S(1)}, u32[]{:S(2)}, u32[]{:S(2)}) async-start(bf16[8,256,128]{2,1,0:T(8,128)(2,1)} %attention.3), calls=%async_computation.4 | async-start | bytes 1048576 | tf_op jit(solution)/shard_map/all_to_all | solution.py:484
  204.0 0.8 copy.25.accept
  204.8 17.2 %all-to-all-done.4.att = bf16[8,256,128]{2,1,0:T(8,128)(2,1)S(1)} async-done(((bf16[8,256,128]{2,1,0:T(8,128)(2,1)}), bf16[8,256,128]{2,1,0:T(8,128)(2,1)S(1)}, u32[]{:S(2)}, u32[]{:S(2)}) %all-to-all-start.4) | async-done | bytes 524320 | tf_op jit(solution)/shard_map/all_to_all | solution.py:484
  222.0 0.0 copy-start.3
  222.0 0.8 copy-done.3
  222.8 13.0 %feed_forward.3 = bf16[1,256,128]{2,1,0:T(8,128)(2,1)} custom-call(s32[2]{0:T(128)} %pad_add_fusion.1.place, bf16[8,256,128]{2,1,0:T(8,128)(2,1)} %copy-done.3, bf16[8,256,128]{2,1,0:T(8,128)(2,1)} %feed_forward.2.refs_0_.x_ref, s32[256,1]{1,0:T(8,128)} %copy.25.accept, bf16[8,320,1024]{2,1,0:T(8,128)(2,1)} %bitcast.70, ...), custom_call_target="tpu_custom_call" | custom-call | tf_op jit(solution)/shard_map/feed_forward/pallas_call | solution.py:460
  (14 shorter events, 0.2 us)
Async XLA Ops:
  6.5 7.6 %copy-start = (bf16[512,1024]{1,0:T(8,128)(2,1)S(1)}, bf16[512,1024]{1,0:T(8,128)(2,1)}, u32[]{:S(2)}) copy-start(bf16[512,1024]{1,0:T(8,128)(2,1)} %param.26) | copy-start | bytes 3145732
  6.5 145.1 %all-gather.6.cloned.1.call-start = ((), (), s32[]{:S(2)}) async-start(), calls=%async_computation.5 | async-start | bytes 5898240 | tf_op jit(solution)/shard_map/all_gather | solution.py:526
  7.2 7.0 %copy-start.7 = (bf16[128,1024]{1,0:T(8,128)(2,1)S(1)}, bf16[128,1024]{1,0:T(8,128)(2,1)}, u32[]{:S(2)}) copy-start(bf16[128,1024]{1,0:T(8,128)(2,1)} %param.24) | copy-start | bytes 786436
  15.1 8.8 %copy-start.5 = (bf16[1024,512]{1,0:T(8,128)(2,1)S(1)}, bf16[1024,512]{1,0:T(8,128)(2,1)}, u32[]{:S(2)}) copy-start(bf16[1024,512]{1,0:T(8,128)(2,1)} %param.25) | copy-start | bytes 3145732
  15.1 9.7 %copy-start.4 = (s32[32,64]{1,0:T(8,128)S(1)}, s32[32,64]{1,0:T(8,128)}, u32[]{:S(2)}) copy-start(s32[32,64]{1,0:T(8,128)} %page_table.1) | copy-start | bytes 24580
  15.1 14.6 %copy-start.6 = (bf16[256,128]{1,0:T(8,128)(2,1)S(1)}, bf16[256,128]{1,0:T(8,128)(2,1)}, u32[]{:S(2)}) copy-start(bf16[256,128]{1,0:T(8,128)(2,1)} %param.19) | copy-start | bytes 196612
  15.2 62.7 %all-to-all-start.1 = ((bf16[32,2,2,128,128]{4,3,2,1,0:T(8,128)(2,1)}), bf16[32,2,2,128,128]{4,3,2,1,0:T(8,128)(2,1)}, u32[]{:S(2)}, u32[]{:S(2)}) async-start(bf16[32,2,2,128,128]{4,3,2,1,0:T(8,128)(2,1)} %bitcast.72), calls=%async_computation.1 | async-start | bytes 8388608 | tf_op jit(solution)/shard_map/all_to_all | solution.py:198
  23.9 128.3 %all-gather.8.cloned.1.call-start = ((), (), s32[]{:S(2)}) async-start(), calls=%async_computation.6 | async-start | bytes 4718592 | tf_op jit(solution)/shard_map/all_gather | solution.py:525
  77.9 5.4 %copy-start.1 = (bf16[64,128,128]{2,1,0:T(8,128)(2,1)S(1)}, bf16[64,128,128]{2,1,0:T(8,128)(2,1)}, u32[]{:S(2)}) copy-start(bf16[64,128,128]{2,1,0:T(8,128)(2,1)} %keys.1) | copy-start | bytes 6291460
  83.3 6.8 %copy-start.10 = (s32[32]{0:T(128)S(1)}, s32[32]{0:T(128)}, u32[]{:S(2)}) copy-start(s32[32]{0:T(128)} %param.33) | copy-start | bytes 388
  83.3 60.8 %all-to-all-start.2 = ((bf16[32,2,2,128,128]{4,3,2,1,0:T(8,128)(2,1)}), bf16[32,2,2,128,128]{4,3,2,1,0:T(8,128)(2,1)}, u32[]{:S(2)}, u32[]{:S(2)}) async-start(bf16[32,2,2,128,128]{4,3,2,1,0:T(8,128)(2,1)} %bitcast.66), calls=%async_computation.2 | async-start | bytes 8388608 | tf_op jit(solution)/shard_map/all_to_all | solution.py:198
  90.1 70.6 %copy-start.9 = (s32[2,256]{1,0:T(2,128)S(1)}, s32[2,256]{1,0:T(2,128)}, u32[]{:S(2)}) copy-start(s32[2,256]{1,0:T(2,128)} %param.35) | copy-start | bytes 6148
  151.7 26.9 %collective-permute-start = (bf16[8,320,1024]{2,1,0:T(8,128)(2,1)}, bf16[8,320,1024]{2,1,0:T(8,128)(2,1)}, u32[]{:S(2)}, u32[]{:S(2)}) collective-permute-start(bf16[8,320,1024]{2,1,0:T(8,128)(2,1)} %bitcast.67), channel_id=1, source_target_pairs={{0,8},{8,0},{16,24},{24,16},{32,40},{40,32},{48,56},{56,48},{64,72... | collective-permute-start | bytes 15728648 | tf_op jit(solution)/shard_map/ppermute | solution.py:539
  152.1 26.5 %collective-permute-start.1 = (bf16[8,1024,256]{2,1,0:T(8,128)(2,1)}, bf16[8,1024,256]{2,1,0:T(8,128)(2,1)}, u32[]{:S(2)}, u32[]{:S(2)}) collective-permute-start(bf16[8,1024,256]{2,1,0:T(8,128)(2,1)} %bitcast.73), channel_id=1, source_target_pairs={{0,8},{8,0},{16,24},{24,16},{32,40},{40,32},{48,56},{56,48},{64,72... | collective-permute-start | bytes 12582920 | tf_op jit(solution)/shard_map/ppermute | solution.py:538
  152.5 26.2 %all-to-all-start.3 = ((bf16[8,256,128]{2,1,0:T(8,128)(2,1)}), bf16[8,256,128]{2,1,0:T(8,128)(2,1)S(1)}, u32[]{:S(2)}, u32[]{:S(2)}) async-start(bf16[8,256,128]{2,1,0:T(8,128)(2,1)} %attention.2), calls=%async_computation.3 | async-start | bytes 1048576 | tf_op jit(solution)/shard_map/all_to_all | solution.py:484
  178.6 0.8 copy-start.2
  200.5 21.5 %all-to-all-start.4 = ((bf16[8,256,128]{2,1,0:T(8,128)(2,1)}), bf16[8,256,128]{2,1,0:T(8,128)(2,1)S(1)}, u32[]{:S(2)}, u32[]{:S(2)}) async-start(bf16[8,256,128]{2,1,0:T(8,128)(2,1)} %attention.3), calls=%async_computation.4 | async-start | bytes 1048576 | tf_op jit(solution)/shard_map/all_to_all | solution.py:484
  222.0 0.8 copy-start.3
Sparse Core Ops, SparseCore 0:
  15.2 73.0 all-gather.5
  90.2 53.3 all-gather.7

commit v3 on v2

--- a/solution.py
+++ b/solution.py
@@ -375,7 +375,7 @@
 def ffn_kernel(
     place,
     att,
-    x_ref,
+    x_in,
     accept,
     low_a,
     low_b,
@@ -392,7 +392,10 @@
     hidden,
     acc,
     w_out,
+    x_ref,
     w_sem,
+    a_sem,
+    x_sem,
 ):
     step = pl.program_id(0)
     shards, rows, width = x_ref.shape
@@ -401,16 +404,18 @@
 
     @pl.when(step == 0)
     def _():
+        pltpu.make_async_copy(x_in, x_ref, x_sem).start()
         half = width // 2
         skip = down_a.shape[1]
         for i in range(shards):
             for low, owner in ((low_a, core), (low_b, 1 - core)):
                 at = pl.ds(pl.multiple_of(i * width + owner * half, half), half)
                 pltpu.make_async_copy(low.at[i, skip : skip + half], w_out.at[at], w_sem).start()
-        for i in range(shards):
-            wide[:, i * width : (i + 1) * width] = att[i]
+            pltpu.make_async_copy(att.at[i], wide.at[:, i * width : (i + 1) * width], a_sem).start()
+        pltpu.make_async_copy(wide, wide, a_sem).wait()
         pltpu.make_async_copy(w_out, w_out, w_sem).wait()
         total = jnp.dot(wide[...], w_out[...], preferred_element_type=F32)
+        pltpu.make_async_copy(x_in, x_ref, x_sem).wait()
         for i in range(shards):
             wide[:, i * width : (i + 1) * width] = x_ref[i]
         total = total + wide[...].astype(F32)
@@ -461,7 +466,7 @@
         ffn_kernel,
         grid=(shards // PER,),
         out_shape=jax.ShapeDtypeStruct((outs, rows, width), BF16),
-        in_specs=[SMEM, fixed(x_parts.shape), fixed(x_parts.shape), fixed((rows, 1)), ANY, ANY]
+        in_specs=[SMEM, ANY, ANY, fixed((rows, 1)), ANY, ANY]
         + [part(full, units)] * 2
         + [part(units, full)] * 2
         + [fixed((1, full))] * 4,
@@ -471,6 +476,9 @@
             pltpu.VMEM((rows, full), BF16),
             pltpu.VMEM((rows, full), F32),
             pltpu.VMEM((full, full), BF16),
+            pltpu.VMEM(x_parts.shape, BF16),
+            pltpu.SemaphoreType.DMA,
+            pltpu.SemaphoreType.DMA,
             pltpu.SemaphoreType.DMA,
         ],
         compiler_params=pltpu.CompilerParams(
@@ -533,9 +541,10 @@
             place, outs, to_all(attention), x_parts, taken.reshape(rows, 1), up, low, *norms
         )
 
+    up = (up_mine, lax.ppermute(up_mine, "pages", core_pair()))
+    pages, up = lax.optimization_barrier((pages, up))
     attention = attend(found, length, shards, project_all(x_parts, *projections), pages)
     attention, low_mine = lax.optimization_barrier((attention, low_mine))
-    up = (up_mine, lax.ppermute(up_mine, "pages", core_pair()))
     low = (low_mine, lax.ppermute(low_mine, "pages", core_pair()))
     middle = layer(shards, attention, x_parts, accept[0], up, low)
     attention = attend(found, length, shards, (middle,) + projections, pages)

time: 247 us -> 247 us (level)
  the two profiles are of different devices: /device:TPU:9 before, /device:TPU:25 now
where the time goes in v3:
time: 247 us; the launch traced here: 245 us
  waiting for transfers between devices  97.5 us (39%)
  Pallas kernels  64.4 us (26%)
  blocking collectives  28.6 us (12%)
  starting transfers between devices  27.8 us (11%)
  between operations  14.4 us (6%)
  other arithmetic  6.4 us (3%)
  local copies, waits for them, and re-layouts  5.56 us (2%)
    all_to_all x2, waiting for transfers between devices, exchange(): lax.all_to_all(pages.reshape((holders, shape[0] // holders) + shape[1:]),...  66.7 us
    all_to_all x2, waiting for transfers between devices, to_all(): return lax.all_to_all(copies, 'mlp', 0, 0, tiled=True)  30.7 us
    all_gather x1, blocking collectives, pages_to_owners(): x_parts = lax.all_gather(later[0], 'mlp', axis=0)  28.6 us
    pallas_call x2, Pallas kernels, feed_forward(): pl.pallas_call(ffn_kernel, grid=(shards // PER,), out_shape=jax.ShapeDtyp...  26.5 us
    pallas_call x2, Pallas kernels, attend(): pl.pallas_call(functools.partial(attention_kernel, inner), out_shape=jax....  21.8 us
    all_to_all x2, starting transfers between devices, exchange(): lax.all_to_all(pages.reshape((holders, shape[0] // holders) + shape[1:]),...  15.9 us
    all_to_all x2, starting transfers between devices, to_all(): return lax.all_to_all(copies, 'mlp', 0, 0, tiled=True)  11.7 us
    pallas_call x1, Pallas kernels, pack_pages(): pl.pallas_call(pack_kernel, out_shape=jax.ShapeDtypeStruct(shape, BF16),...  7.29 us
  transfers between devices with their start and end apart: 8, of which 4 were waited for; matrix products, arithmetic and copies ran while one was open for 4% of the time, Pallas kernels for 8%

profile of v3, /device:TPU:25, one launch (start us, length us, event | category | flops | bytes accessed | tf_op | source)
XLA Modules:
  0.0 244.7 jit_solution(12948791405665150866)
XLA Ops:
  6.5 0.0 copy-start
  6.5 0.0 all-gather.6.cloned.1.call-start
  6.5 0.7 pad_add_fusion.2.where_and_turn
  7.2 7.3 %pack_pages.7 = bf16[64,2,128,128]{3,2,1,0:T(8,128)(2,1)} custom-call(s32[2]{0:T(128)} %pad_add_fusion.2.where_and_turn, s32[32,64]{1,0:T(8,128)} %page_table.1, bf16[64,128,128]{2,1,0:T(8,128)(2,1)} %keys.1, bf16[64,128,128]{2,1,0:T(8,128)(2,1)} %values.1), custom_call_target="tpu_custom_call" | custom-call | tf_op jit(solution)/shard_map/pack_pages/pallas_call | solution.py:166
  14.5 0.0 copy-done
  14.5 0.8 constant_dynamic-slice_fusion.2
  15.4 0.0 all-gather.6.cloned.1.call-update
  15.4 0.0 copy-start.7
  15.4 0.0 copy-start.5
  15.4 0.0 copy-start.4
  15.4 0.0 copy-start.6
  15.4 8.0 %all-to-all-start.1 = ((bf16[32,2,2,128,128]{4,3,2,1,0:T(8,128)(2,1)}), bf16[32,2,2,128,128]{4,3,2,1,0:T(8,128)(2,1)}, u32[]{:S(2)}, u32[]{:S(2)}) async-start(bf16[32,2,2,128,128]{4,3,2,1,0:T(8,128)(2,1)} %bitcast.72), calls=%async_computation.1 | async-start | bytes 8388608 | tf_op jit(solution)/shard_map/all_to_all | solution.py:198
  23.4 0.0 all-gather.8.cloned.1.call-start
  23.5 0.0 copy-done.7
  23.5 0.0 copy-done.5
  23.6 0.9 pad_maximum_fusion
  24.5 0.0 all-gather.8.cloned.1.call-update
  24.5 0.0 copy-done.4
  24.6 1.2 convert_reduce_fusion.2
  25.7 0.8 convert_reduce_fusion.3
  26.5 0.3 convert_reduce_fusion
  26.9 0.7 reduce_max.9
  28.2 0.2 convert_reduce_fusion.1
  28.5 0.1 select_reduce_fusion.2
  28.7 0.1 copy.23
  28.7 0.7 sub.64.table
  29.4 0.0 copy-done.6
  29.4 28.6 %all-gather = bf16[2048,128]{1,0:T(8,128)(2,1)} all-gather(bf16[256,128]{1,0:T(8,128)(2,1)S(1)} %copy-done.6), channel_id=2, replica_groups=mesh['pages'=32,'mlp'=8] {'mlp'}, dimensions={0}, use_global_device_ids=true | all-gather | bytes 589824 | tf_op jit(solution)/shard_map/all_gather | solution.py:211
  58.1 18.1 %all-to-all-done.1 = bf16[32,2,2,128,128]{4,3,2,1,0:T(8,128)(2,1)} async-done(((bf16[32,2,2,128,128]{4,3,2,1,0:T(8,128)(2,1)}), bf16[32,2,2,128,128]{4,3,2,1,0:T(8,128)(2,1)}, u32[]{:S(2)}, u32[]{:S(2)}) %all-to-all-start.1) | async-done | bytes 4194336 | tf_op jit(solution)/shard_map/all_to_all | solution.py:198
  76.2 0.0 copy-start.1
  76.2 6.1 %repack_pages.7 = bf16[64,2,128,128]{3,2,1,0:T(8,128)(2,1)} custom-call(s32[64]{0:T(128)} %sub.64.table, bf16[64,2,128,128]{3,2,1,0:T(8,128)(2,1)} %bitcast.6.got), custom_call_target="tpu_custom_call" | custom-call | tf_op jit(solution)/shard_map/repack_pages/pallas_call | solution.py:184
  82.4 0.0 all-gather.6.cloned.1.call-done
  82.4 0.1 collective-permute-start
  82.5 0.0 copy-done.1
  82.5 0.0 copy-start.10
  82.5 7.9 %all-to-all-start.2 = ((bf16[32,2,2,128,128]{4,3,2,1,0:T(8,128)(2,1)}), bf16[32,2,2,128,128]{4,3,2,1,0:T(8,128)(2,1)}, u32[]{:S(2)}, u32[]{:S(2)}) async-start(bf16[32,2,2,128,128]{4,3,2,1,0:T(8,128)(2,1)} %bitcast.66), calls=%async_computation.2 | async-start | bytes 8388608 | tf_op jit(solution)/shard_map/all_to_all | solution.py:198
  90.4 0.0 copy-start.9
  90.4 0.0 copy-done.10
  90.4 0.6 dynamic_slice.20.length
  91.0 0.2 convert_reduce_fusion.4
  91.2 0.1 select_reduce_fusion.3
  91.3 0.6 compare_select_fusion.1.found
  91.9 2.7 %project.1 = (bf16[512,128]{1,0:T(8,128)(2,1)}, bf16[512,128]{1,0:T(8,128)(2,1)}, bf16[256,128]{1,0:T(8,128)(2,1)}, bf16[256,128]{1,0:T(8,128)(2,1)}) custom-call(bf16[8,256,128]{2,1,0:T(8,128)(2,1)} %bitcast.76, bf16[1024,128]{1,0:T(8,128)(2,1)} %refs_1_.1, bf16[1024,128]{1,0:T(8,128)(2,1)} %refs_2_.1, bf16[1024,128]{1,0:T(8,128)(2,1)} %refs_3_.1, ...), custom_call_target="tpu_custom_call" | custom-call | tf_op jit(solution)/shard_map/project/pallas_call | solution.py:251
  94.6 48.6 %all-to-all-done.2 = bf16[32,2,2,128,128]{4,3,2,1,0:T(8,128)(2,1)} async-done(((bf16[32,2,2,128,128]{4,3,2,1,0:T(8,128)(2,1)}), bf16[32,2,2,128,128]{4,3,2,1,0:T(8,128)(2,1)}, u32[]{:S(2)}, u32[]{:S(2)}) %all-to-all-start.2) | async-done | bytes 4194336 | tf_op jit(solution)/shard_map/all_to_all | solution.py:198
  143.2 0.0 collective-permute-done.up_b
  143.2 10.8 %attention.2 = bf16[8,256,128]{2,1,0:T(8,128)(2,1)} custom-call(s32[64]{0:T(128)} %compare_select_fusion.1.found, s32[1]{0:T(128)} %dynamic_slice.20.length, bf16[512,128]{1,0:T(8,128)(2,1)} %get-tuple-element.307.refs_0_, bf16[512,128]{1,0:T(8,128)(2,1)} %get-tuple-element.308.refs_1_, bf16[256,128]{1,0:T(8,128)(2,1)} %get-tuple-element.309.refs_2_, ...), custom_call_target="tpu_custom_call" | custom-call | tf_op jit(solution)/shard_map/attention/pallas_call | solution.py:357
  154.0 0.0 all-gather.8.cloned.1.call-done
  154.0 0.1 collective-permute-start.1
  154.1 8.2 %all-to-all-start.3 = ((bf16[8,256,128]{2,1,0:T(8,128)(2,1)}), bf16[8,256,128]{2,1,0:T(8,128)(2,1)S(1)}, u32[]{:S(2)}, u32[]{:S(2)}) async-start(bf16[8,256,128]{2,1,0:T(8,128)(2,1)} %attention.2), calls=%async_computation.3 | async-start | bytes 1048576 | tf_op jit(solution)/shard_map/all_to_all | solution.py:492
  162.3 0.0 copy-done.9
  162.4 0.8 copy.24.accept
  163.2 0.6 pad_add_fusion.1.place
  163.8 16.5 %all-to-all-done.3.att = bf16[8,256,128]{2,1,0:T(8,128)(2,1)S(1)} async-done(((bf16[8,256,128]{2,1,0:T(8,128)(2,1)}), bf16[8,256,128]{2,1,0:T(8,128)(2,1)S(1)}, u32[]{:S(2)}, u32[]{:S(2)}) %all-to-all-start.3) | async-done | bytes 524320 | tf_op jit(solution)/shard_map/all_to_all | solution.py:492
  180.3 0.0 copy-start.2
  180.3 0.0 collective-permute-done.1.low_b.down_b
  180.3 0.8 copy-done.2
  181.1 13.3 %feed_forward.2.refs_0_.x_in = bf16[8,256,128]{2,1,0:T(8,128)(2,1)} custom-call(s32[2]{0:T(128)} %pad_add_fusion.1.place, bf16[8,256,128]{2,1,0:T(8,128)(2,1)} %copy-done.2, bf16[8,256,128]{2,1,0:T(8,128)(2,1)} %bitcast.77, s32[256,1]{1,0:T(8,128)} %copy.24.accept, bf16[8,320,1024]{2,1,0:T(8,128)(2,1)} %bitcast.68, ...), custom_call_target="tpu_custom_call" | custom-call | tf_op jit(solution)/shard_map/feed_forward/pallas_call | solution.py:465
  194.4 11.0 %attention.3 = bf16[8,256,128]{2,1,0:T(8,128)(2,1)} custom-call(s32[64]{0:T(128)} %compare_select_fusion.1.found, s32[1]{0:T(128)} %dynamic_slice.20.length, bf16[8,256,128]{2,1,0:T(8,128)(2,1)} %feed_forward.2.refs_0_.x_in, bf16[1024,128]{1,0:T(8,128)(2,1)} %refs_1_.1, bf16[1024,128]{1,0:T(8,128)(2,1)} %refs_2_.1, bf16[1024,128]{1,0:T(8,128)(2,1)} %refs_3_.1, ...), custom_call_target="tpu_custom_call" | custom-call | tf_op jit(solution)/shard_map/attention/pallas_call | solution.py:357
  205.4 3.5 %all-to-all-start.4 = ((bf16[8,256,128]{2,1,0:T(8,128)(2,1)}), bf16[8,256,128]{2,1,0:T(8,128)(2,1)S(1)}, u32[]{:S(2)}, u32[]{:S(2)}) async-start(bf16[8,256,128]{2,1,0:T(8,128)(2,1)} %attention.3), calls=%async_computation.4 | async-start | bytes 1048576 | tf_op jit(solution)/shard_map/all_to_all | solution.py:492
  208.9 0.8 copy.25.accept
  209.7 14.2 %all-to-all-done.4.att = bf16[8,256,128]{2,1,0:T(8,128)(2,1)S(1)} async-done(((bf16[8,256,128]{2,1,0:T(8,128)(2,1)}), bf16[8,256,128]{2,1,0:T(8,128)(2,1)S(1)}, u32[]{:S(2)}, u32[]{:S(2)}) %all-to-all-start.4) | async-done | bytes 524320 | tf_op jit(solution)/shard_map/all_to_all | solution.py:492
  223.9 0.0 copy-start.3
  223.9 0.8 copy-done.3
  224.7 13.2 %feed_forward.3 = bf16[1,256,128]{2,1,0:T(8,128)(2,1)} custom-call(s32[2]{0:T(128)} %pad_add_fusion.1.place, bf16[8,256,128]{2,1,0:T(8,128)(2,1)} %copy-done.3, bf16[8,256,128]{2,1,0:T(8,128)(2,1)} %feed_forward.2.refs_0_.x_in, s32[256,1]{1,0:T(8,128)} %copy.25.accept, bf16[8,320,1024]{2,1,0:T(8,128)(2,1)} %bitcast.70, ...), custom_call_target="tpu_custom_call" | custom-call | tf_op jit(solution)/shard_map/feed_forward/pallas_call | solution.py:465
  (14 shorter events, 0.2 us)
Async XLA Ops:
  6.5 8.0 %copy-start = (bf16[1024,512]{1,0:T(8,128)(2,1)S(1)}, bf16[1024,512]{1,0:T(8,128)(2,1)}, u32[]{:S(2)}) copy-start(bf16[1024,512]{1,0:T(8,128)(2,1)} %param.25) | copy-start | bytes 3145732
  6.5 75.8 %all-gather.6.cloned.1.call-start = ((), (), s32[]{:S(2)}) async-start(), calls=%async_computation.5 | async-start | bytes 4718592 | tf_op jit(solution)/shard_map/all_gather | solution.py:533
  15.4 8.1 %copy-start.7 = (bf16[128,1024]{1,0:T(8,128)(2,1)S(1)}, bf16[128,1024]{1,0:T(8,128)(2,1)}, u32[]{:S(2)}) copy-start(bf16[128,1024]{1,0:T(8,128)(2,1)} %param.24) | copy-start | bytes 786436
  15.4 8.1 %copy-start.5 = (bf16[512,1024]{1,0:T(8,128)(2,1)S(1)}, bf16[512,1024]{1,0:T(8,128)(2,1)}, u32[]{:S(2)}) copy-start(bf16[512,1024]{1,0:T(8,128)(2,1)} %param.26) | copy-start | bytes 3145732
  15.4 9.1 %copy-start.4 = (s32[32,64]{1,0:T(8,128)S(1)}, s32[32,64]{1,0:T(8,128)}, u32[]{:S(2)}) copy-start(s32[32,64]{1,0:T(8,128)} %page_table.1) | copy-start | bytes 24580
  15.4 14.0 %copy-start.6 = (bf16[256,128]{1,0:T(8,128)(2,1)S(1)}, bf16[256,128]{1,0:T(8,128)(2,1)}, u32[]{:S(2)}) copy-start(bf16[256,128]{1,0:T(8,128)(2,1)} %param.19) | copy-start | bytes 196612
  15.4 60.8 %all-to-all-start.1 = ((bf16[32,2,2,128,128]{4,3,2,1,0:T(8,128)(2,1)}), bf16[32,2,2,128,128]{4,3,2,1,0:T(8,128)(2,1)}, u32[]{:S(2)}, u32[]{:S(2)}) async-start(bf16[32,2,2,128,128]{4,3,2,1,0:T(8,128)(2,1)} %bitcast.72), calls=%async_computation.1 | async-start | bytes 8388608 | tf_op jit(solution)/shard_map/all_to_all | solution.py:198
  23.4 130.6 %all-gather.8.cloned.1.call-start = ((), (), s32[]{:S(2)}) async-start(), calls=%async_computation.6 | async-start | bytes 5898240 | tf_op jit(solution)/shard_map/all_gather | solution.py:534
  76.2 6.3 %copy-start.1 = (bf16[64,128,128]{2,1,0:T(8,128)(2,1)S(1)}, bf16[64,128,128]{2,1,0:T(8,128)(2,1)}, u32[]{:S(2)}) copy-start(bf16[64,128,128]{2,1,0:T(8,128)(2,1)} %keys.1) | copy-start | bytes 6291460
  82.4 60.8 %collective-permute-start = (bf16[8,1024,256]{2,1,0:T(8,128)(2,1)}, bf16[8,1024,256]{2,1,0:T(8,128)(2,1)}, u32[]{:S(2)}, u32[]{:S(2)}) collective-permute-start(bf16[8,1024,256]{2,1,0:T(8,128)(2,1)} %bitcast.73), channel_id=1, source_target_pairs={{0,8},{8,0},{16,24},{24,16},{32,40},{40,32},{48,56},{56,48},{64,72... | collective-permute-start | bytes 12582920 | tf_op jit(solution)/shard_map/ppermute | solution.py:544
  82.5 7.9 %copy-start.10 = (s32[32]{0:T(128)S(1)}, s32[32]{0:T(128)}, u32[]{:S(2)}) copy-start(s32[32]{0:T(128)} %param.33) | copy-start | bytes 388
  82.5 60.6 %all-to-all-start.2 = ((bf16[32,2,2,128,128]{4,3,2,1,0:T(8,128)(2,1)}), bf16[32,2,2,128,128]{4,3,2,1,0:T(8,128)(2,1)}, u32[]{:S(2)}, u32[]{:S(2)}) async-start(bf16[32,2,2,128,128]{4,3,2,1,0:T(8,128)(2,1)} %bitcast.66), calls=%async_computation.2 | async-start | bytes 8388608 | tf_op jit(solution)/shard_map/all_to_all | solution.py:198
  90.4 71.9 %copy-start.9 = (s32[2,256]{1,0:T(2,128)S(1)}, s32[2,256]{1,0:T(2,128)}, u32[]{:S(2)}) copy-start(s32[2,256]{1,0:T(2,128)} %param.35) | copy-start | bytes 6148
  154.0 26.3 %collective-permute-start.1 = (bf16[8,320,1024]{2,1,0:T(8,128)(2,1)}, bf16[8,320,1024]{2,1,0:T(8,128)(2,1)}, u32[]{:S(2)}, u32[]{:S(2)}) collective-permute-start(bf16[8,320,1024]{2,1,0:T(8,128)(2,1)} %bitcast.67), channel_id=1, source_target_pairs={{0,8},{8,0},{16,24},{24,16},{32,40},{40,32},{48,56},{56,48},{64,72... | collective-permute-start | bytes 15728648 | tf_op jit(solution)/shard_map/ppermute | solution.py:548
  154.1 26.2 %all-to-all-start.3 = ((bf16[8,256,128]{2,1,0:T(8,128)(2,1)}), bf16[8,256,128]{2,1,0:T(8,128)(2,1)S(1)}, u32[]{:S(2)}, u32[]{:S(2)}) async-start(bf16[8,256,128]{2,1,0:T(8,128)(2,1)} %attention.2), calls=%async_computation.3 | async-start | bytes 1048576 | tf_op jit(solution)/shard_map/all_to_all | solution.py:492
  180.3 0.8 copy-start.2
  205.4 18.5 %all-to-all-start.4 = ((bf16[8,256,128]{2,1,0:T(8,128)(2,1)}), bf16[8,256,128]{2,1,0:T(8,128)(2,1)S(1)}, u32[]{:S(2)}, u32[]{:S(2)}) async-start(bf16[8,256,128]{2,1,0:T(8,128)(2,1)} %attention.3), calls=%async_computation.4 | async-start | bytes 1048576 | tf_op jit(solution)/shard_map/all_to_all | solution.py:492
  223.9 0.8 copy-start.3
Sparse Core Ops, SparseCore 0:
  15.5 62.6 all-gather.5
  80.0 63.2 all-gather.7

commit v4 on v2

--- a/solution.py
+++ b/solution.py
@@ -360,7 +360,7 @@
         in_specs=[SMEM, SMEM] + [VMEM] * len(given) + [ANY],
         out_specs=VMEM,
         scratch_shapes=scratch,
-        compiler_params=pltpu.CompilerParams(vmem_limit_bytes=56 << 20),
+        compiler_params=pltpu.CompilerParams(vmem_limit_bytes=(50 if inner else 56) << 20),
         name="attention",
     )(found, length, *given, pages)
 
@@ -373,12 +373,11 @@
 
 
 def ffn_kernel(
-    place,
+    column,
     att,
     x_ref,
     accept,
-    low_a,
-    low_b,
+    w_out,
     up_a,
     up_b,
     down_a,
@@ -391,25 +390,15 @@
     wide,
     hidden,
     acc,
-    w_out,
-    w_sem,
 ):
     step = pl.program_id(0)
     shards, rows, width = x_ref.shape
     full = shards * width
-    column, core = place[0], place[1]
 
     @pl.when(step == 0)
     def _():
-        half = width // 2
-        skip = down_a.shape[1]
-        for i in range(shards):
-            for low, owner in ((low_a, core), (low_b, 1 - core)):
-                at = pl.ds(pl.multiple_of(i * width + owner * half, half), half)
-                pltpu.make_async_copy(low.at[i, skip : skip + half], w_out.at[at], w_sem).start()
         for i in range(shards):
             wide[:, i * width : (i + 1) * width] = att[i]
-        pltpu.make_async_copy(w_out, w_out, w_sem).wait()
         total = jnp.dot(wide[...], w_out[...], preferred_element_type=F32)
         for i in range(shards):
             wide[:, i * width : (i + 1) * width] = x_ref[i]
@@ -441,12 +430,12 @@
         else:
             for i in range(shards):
 
-                @pl.when(column == i)
+                @pl.when(column[0] == i)
                 def _():
                     out[0] = jnp.where(chosen, result[:, i * width : (i + 1) * width], x_ref[i])
 
 
-def feed_forward(place, outs, att, x_parts, accept, up, low, g1, b1, g2, b2):
+def feed_forward(column, outs, att, x_parts, accept, w_out, up, down, g1, b1, g2, b2):
     shards, rows, width = x_parts.shape
     full = shards * width
     units = up[0].shape[2]
@@ -461,7 +450,8 @@
         ffn_kernel,
         grid=(shards // PER,),
         out_shape=jax.ShapeDtypeStruct((outs, rows, width), BF16),
-        in_specs=[SMEM, fixed(x_parts.shape), fixed(x_parts.shape), fixed((rows, 1)), ANY, ANY]
+        in_specs=[SMEM, fixed(x_parts.shape), fixed(x_parts.shape), fixed((rows, 1))]
+        + [fixed(w_out.shape)]
         + [part(full, units)] * 2
         + [part(units, full)] * 2
         + [fixed((1, full))] * 4,
@@ -470,14 +460,12 @@
             pltpu.VMEM((rows, full), BF16),
             pltpu.VMEM((rows, full), BF16),
             pltpu.VMEM((rows, full), F32),
-            pltpu.VMEM((full, full), BF16),
-            pltpu.SemaphoreType.DMA,
         ],
         compiler_params=pltpu.CompilerParams(
-            dimension_semantics=("arbitrary",), vmem_limit_bytes=60 << 20
+            dimension_semantics=("arbitrary",), vmem_limit_bytes=52 << 20
         ),
         name="feed_forward",
-    )(place, att, x_parts, accept, *low, *up, *low, g1, b1, g2, b2)
+    )(column, att, x_parts, accept, w_out, *up, *down, g1, b1, g2, b2)
 
 
 def to_all(copies):
@@ -511,35 +499,53 @@
     me = lax.axis_index("pages")
     shard = lax.axis_index("mlp")
     rows, width = embeddings.shape
-    pages, found, x_parts, (w_up, w_down, w_out) = pages_to_owners(
-        page_table, cache_keys, cache_values, (embeddings, w_up, w_down, w_out)
+    core = me % 2
+    half_out = w_out.shape[0] // 2
+    out_half = lax.dynamic_slice_in_dim(w_out, core * half_out, half_out, 0)
+    out_mine = lax.all_gather(out_half, "mlp", axis=0)
+    pages, found, x_parts, (w_up, w_down) = pages_to_owners(
+        page_table, cache_keys, cache_values, (embeddings, w_up, w_down)
     )
     length = lax.dynamic_slice_in_dim(lengths, me, 1, 0)
 
-    core = me % 2
     half = w_up.shape[1] // 2
-    half_out = w_out.shape[0] // 2
     up_half = lax.dynamic_slice_in_dim(w_up, core * half, half, 1)
     down_half = lax.dynamic_slice_in_dim(w_down, core * half, half, 0)
-    out_half = lax.dynamic_slice_in_dim(w_out, core * half_out, half_out, 0)
     up_mine = lax.all_gather(up_half, "mlp", axis=0)
-    low_mine = lax.all_gather(jnp.concatenate([down_half, out_half]), "mlp", axis=0)
+    down_mine = lax.all_gather(down_half, "mlp", axis=0)
     norms = [v.reshape(1, -1) for v in (norm1_gain, norm1_bias, norm2_gain, norm2_bias)]
-    place = jnp.stack([shard, core]).astype(jnp.int32)
+    column = shard.reshape(1).astype(jnp.int32)
     projections = (w_query, w_key, w_value, w_global_query)
 
-    def layer(outs, attention, x_parts, taken, up, low):
+    def swap(array):
+        return lax.ppermute(array, "pages", core_pair())
+
+    out_other = swap(out_mine)
+    w_out_all = jnp.where(
+        core == 0, jnp.stack([out_mine, out_other], 1), jnp.stack([out_other, out_mine], 1)
+    ).reshape(shards * w_out.shape[0], -1)
+    up = (up_mine, swap(up_mine))
+    pages, up, w_out_all = lax.optimization_barrier((pages, up, w_out_all))
+
+    def layer(outs, attention, x_parts, taken, down):
         return feed_forward(
-            place, outs, to_all(attention), x_parts, taken.reshape(rows, 1), up, low, *norms
+            column,
+            outs,
+            to_all(attention),
+            x_parts,
+            taken.reshape(rows, 1),
+            w_out_all,
+            up,
+            down,
+            *norms,
         )
 
     attention = attend(found, length, shards, project_all(x_parts, *projections), pages)
-    attention, low_mine = lax.optimization_barrier((attention, low_mine))
-    up = (up_mine, lax.ppermute(up_mine, "pages", core_pair()))
-    low = (low_mine, lax.ppermute(low_mine, "pages", core_pair()))
-    middle = layer(shards, attention, x_parts, accept[0], up, low)
+    attention, down_mine = lax.optimization_barrier((attention, down_mine))
+    down = (down_mine, swap(down_mine))
+    middle = layer(shards, attention, x_parts, accept[0], down)
     attention = attend(found, length, shards, (middle,) + projections, pages)
-    return layer(1, attention, middle, accept[1], up, low).reshape(rows, width)
+    return layer(1, attention, middle, accept[1], down).reshape(rows, width)
 
 
 def solution(mesh):

time: 247 us -> 257 us (1.040)
  waiting for transfers between devices: 103 us -> 113 us
    all_gather x1 -> x2, waiting for transfers between devices: 0.02 us -> 37.9 us  [the longest x1 20.7 us: per_device(): out_mine = lax.all_gather(out_half, 'mlp', axis=0)]
    all_to_all x2, waiting for transfers between devices: 69.4 us -> 39.7 us  [exchange(): lax.all_to_all(pages.reshape((holders, shape[0] // holders) + shape[1:]),...]
    ppermute x2 -> x3, starting transfers between devices: 0.78 us -> 6.22 us  [swap(): return lax.ppermute(array, 'pages', core_pair())]
    all_to_all x2, starting transfers between devices: 11.7 us -> 7.55 us  [to_all(): return lax.all_to_all(copies, 'mlp', 0, 0, tiled=True)]
    pallas_call x2, Pallas kernels: 26.2 us -> 22.8 us  [feed_forward(): pl.pallas_call(ffn_kernel, grid=(shards // PER,), out_shape=jax.ShapeDtyp...]
    select_n x0 -> x1, other arithmetic: none -> 3.33 us  [per_device(): jnp.where(core == 0, jnp.stack([out_mine, out_other], 1), jnp.stack([out_...]
  transfers between devices with their start and end apart: 8 -> 10, of which waited for: 4 -> 7; matrix products, arithmetic and copies ran while one was open for 4% -> 4% of each run, Pallas kernels for 6% -> 7%
where the time goes in v4:
time: 257 us; the launch traced here: 253 us
  waiting for transfers between devices  113 us (44%)
  Pallas kernels  56.2 us (22%)
  starting transfers between devices  29.4 us (11%)
  blocking collectives  28.6 us (11%)
  between operations  14.1 us (5%)
  other arithmetic  8.09 us (3%)
  local copies, waits for them, and re-layouts  4.17 us (2%)
    all_to_all x2, waiting for transfers between devices, exchange(): lax.all_to_all(pages.reshape((holders, shape[0] // holders) + shape[1:]),...  39.7 us
    all_to_all x2, waiting for transfers between devices, to_all(): return lax.all_to_all(copies, 'mlp', 0, 0, tiled=True)  34 us
    all_gather x1, blocking collectives, pages_to_owners(): x_parts = lax.all_gather(later[0], 'mlp', axis=0)  28.6 us
    pallas_call x2, Pallas kernels, feed_forward(): pl.pallas_call(ffn_kernel, grid=(shards // PER,), out_shape=jax.ShapeDtyp...  22.8 us
    all_gather x1, waiting for transfers between devices, per_device(): out_mine = lax.all_gather(out_half, 'mlp', axis=0)  20.7 us
    pallas_call x2, Pallas kernels, attend(): pl.pallas_call(functools.partial(attention_kernel, inner), out_shape=jax....  17.4 us
    all_gather x1, waiting for transfers between devices, per_device(): down_mine = lax.all_gather(down_half, 'mlp', axis=0)  17.1 us
    all_to_all x2, starting transfers between devices, exchange(): lax.all_to_all(pages.reshape((holders, shape[0] // holders) + shape[1:]),...  15.5 us
  transfers between devices with their start and end apart: 10, of which 7 were waited for; matrix products, arithmetic and copies ran while one was open for 4% of the time, Pallas kernels for 7%

profile of v4, /device:TPU:9, one launch (start us, length us, event | category | flops | bytes accessed | tf_op | source)
XLA Modules:
  0.0 253.3 jit_solution(5632582159342307056)
XLA Ops:
  6.5 0.0 copy-start
  6.5 0.0 all-gather.8.cloned.1.call-start
  6.5 0.6 pad_add_fusion.1.where_and_turn
  7.1 7.6 %pack_pages.7 = bf16[64,2,128,128]{3,2,1,0:T(8,128)(2,1)} custom-call(s32[2]{0:T(128)} %pad_add_fusion.1.where_and_turn, s32[32,64]{1,0:T(8,128)} %page_table.1, bf16[64,128,128]{2,1,0:T(8,128)(2,1)} %keys.1, bf16[64,128,128]{2,1,0:T(8,128)(2,1)} %values.1), custom_call_target="tpu_custom_call" | custom-call | tf_op jit(solution)/shard_map/pack_pages/pallas_call | solution.py:166
  14.8 0.0 copy-done
  14.8 0.8 constant_dynamic-slice_fusion.2
  15.6 0.0 all-gather.8.cloned.1.call-update
  15.6 0.0 all-gather.10.cloned.1.call-start
  15.7 0.7 constant_dynamic-slice_fusion.1
  16.4 0.0 all-gather.10.cloned.1.call-update
  16.4 0.0 copy-start.13
  16.4 0.0 copy-start.12
  16.4 0.0 copy-start.14
  16.4 8.1 %all-to-all-start.1 = ((bf16[32,2,2,128,128]{4,3,2,1,0:T(8,128)(2,1)}), bf16[32,2,2,128,128]{4,3,2,1,0:T(8,128)(2,1)}, u32[]{:S(2)}, u32[]{:S(2)}) async-start(bf16[32,2,2,128,128]{4,3,2,1,0:T(8,128)(2,1)} %bitcast.90), calls=%async_computation.1 | async-start | bytes 8388608 | tf_op jit(solution)/shard_map/all_to_all | solution.py:198
  24.6 0.0 all-gather.12.cloned.1.call-start
  24.6 0.0 copy-done.13
  24.6 0.8 constant_dynamic-slice_fusion
  25.5 0.0 all-gather.12.cloned.1.call-update
  25.5 1.2 convert_reduce_fusion.2
  26.7 0.8 convert_reduce_fusion.3
  27.5 0.3 convert_reduce_fusion
  27.9 0.6 reduce_max.9
  29.1 0.2 convert_reduce_fusion.1
  29.4 0.1 select_reduce_fusion.2
  29.5 0.1 copy.27
  29.6 0.7 sub.64.table
  30.3 0.0 copy-done.14
  30.3 28.6 %all-gather = bf16[2048,128]{1,0:T(8,128)(2,1)} all-gather(bf16[256,128]{1,0:T(8,128)(2,1)S(1)} %copy-done.14), channel_id=2, replica_groups=mesh['pages'=32,'mlp'=8] {'mlp'}, dimensions={0}, use_global_device_ids=true | all-gather | bytes 589824 | tf_op jit(solution)/shard_map/all_gather | solution.py:211
  59.0 19.6 %all-to-all-done.1 = bf16[32,2,2,128,128]{4,3,2,1,0:T(8,128)(2,1)} async-done(((bf16[32,2,2,128,128]{4,3,2,1,0:T(8,128)(2,1)}), bf16[32,2,2,128,128]{4,3,2,1,0:T(8,128)(2,1)}, u32[]{:S(2)}, u32[]{:S(2)}) %all-to-all-start.1) | async-done | bytes 4194336 | tf_op jit(solution)/shard_map/all_to_all | solution.py:198
  78.6 5.7 %repack_pages.7 = bf16[64,2,128,128]{3,2,1,0:T(8,128)(2,1)} custom-call(s32[64]{0:T(128)} %sub.64.table, bf16[64,2,128,128]{3,2,1,0:T(8,128)(2,1)} %bitcast.5.got), custom_call_target="tpu_custom_call" | custom-call | tf_op jit(solution)/shard_map/repack_pages/pallas_call | solution.py:184
  84.3 0.0 all-gather.8.cloned.1.call-done
  84.4 1.0 collective-permute-start
  85.3 7.4 %all-to-all-start.2 = ((bf16[32,2,2,128,128]{4,3,2,1,0:T(8,128)(2,1)}), bf16[32,2,2,128,128]{4,3,2,1,0:T(8,128)(2,1)}, u32[]{:S(2)}, u32[]{:S(2)}) async-start(bf16[32,2,2,128,128]{4,3,2,1,0:T(8,128)(2,1)} %bitcast.81), calls=%async_computation.2 | async-start | bytes 8388608 | tf_op jit(solution)/shard_map/all_to_all | solution.py:198
  92.8 20.7 %all-gather.10.cloned.1.call-done = bf16[512,1024]{1,0:T(8,128)(2,1)} async-done(((bf16[64,1024]{1,0:T(8,128)(2,1)}), bf16[512,1024]{1,0:T(8,128)(2,1)}) %all-gather.10.cloned.1.call-update) | async-done | bytes 1048592 | tf_op jit(solution)/shard_map/all_gather | solution.py:505
  113.5 4.6 %collective-permute-start.1 = (bf16[8,64,1024]{2,1,0:T(8,128)(2,1)}, bf16[8,64,1024]{2,1,0:T(8,128)(2,1)S(1)}, u32[]{:S(2)}, u32[]{:S(2)}) collective-permute-start(bf16[8,64,1024]{2,1,0:T(8,128)(2,1)} %bitcast.91), channel_id=1, source_target_pairs={{0,8},{8,0},{16,24},{24,16},{32,40},{40,32},{48,56},{56,48},{64,72... | collective-permute-start | bytes 3145736 | tf_op jit(solution)/shard_map/ppermute | solution.py:521
  118.1 0.7 dynamic_slice.20.length
  118.8 0.2 convert_reduce_fusion.4
  118.9 0.1 select_reduce_fusion.3
  119.0 0.6 compare_select_fusion.1.found
  119.6 1.0 collective-permute-done.1
  120.6 3.3 %maximum_select_fusion = bf16[8,2,64,1024]{3,2,1,0:T(8,128)(2,1)} fusion(bf16[8,1,64,1024]{3,2,1,0:T(8,128)(2,1)S(1)} %bitcast.93, bf16[8,1,64,1024]{3,2,1,0:T(8,128)(2,1)} %bitcast.92, pred[]{:T(512)S(6)} %eq.163), kind=kLoop, calls=%fused_computation.27 | loop fusion | flops 3145728 | bytes 4194305 | tf_op jit(solution)/shard_map/jit(_where)/select_n | solution.py:524
  123.9 0.0 copy-start.8
  123.9 0.0 copy-start.9
  124.0 2.8 %project.1 = (bf16[512,128]{1,0:T(8,128)(2,1)}, bf16[512,128]{1,0:T(8,128)(2,1)}, bf16[256,128]{1,0:T(8,128)(2,1)}, bf16[256,128]{1,0:T(8,128)(2,1)}) custom-call(bf16[8,256,128]{2,1,0:T(8,128)(2,1)} %bitcast.70, bf16[1024,128]{1,0:T(8,128)(2,1)} %refs_1_.1, bf16[1024,128]{1,0:T(8,128)(2,1)} %refs_2_.1, bf16[1024,128]{1,0:T(8,128)(2,1)} %refs_3_.1, ...), custom_call_target="tpu_custom_call" | custom-call | tf_op jit(solution)/shard_map/project/pallas_call | solution.py:251
  126.7 20.1 %all-to-all-done.2 = bf16[32,2,2,128,128]{4,3,2,1,0:T(8,128)(2,1)} async-done(((bf16[32,2,2,128,128]{4,3,2,1,0:T(8,128)(2,1)}), bf16[32,2,2,128,128]{4,3,2,1,0:T(8,128)(2,1)}, u32[]{:S(2)}, u32[]{:S(2)}) %all-to-all-start.2) | async-done | bytes 4194336 | tf_op jit(solution)/shard_map/all_to_all | solution.py:198
  146.8 0.0 collective-permute-done.up_b
  146.8 9.0 %attention.2 = bf16[8,256,128]{2,1,0:T(8,128)(2,1)} custom-call(s32[64]{0:T(128)} %compare_select_fusion.1.found, s32[1]{0:T(128)} %dynamic_slice.20.length, bf16[512,128]{1,0:T(8,128)(2,1)} %get-tuple-element.307.refs_0_, bf16[512,128]{1,0:T(8,128)(2,1)} %get-tuple-element.308.refs_1_, bf16[256,128]{1,0:T(8,128)(2,1)} %get-tuple-element.309.refs_2_, ...), custom_call_target="tpu_custom_call" | custom-call | tf_op jit(solution)/shard_map/attention/pallas_call | solution.py:357
  155.8 17.1 %all-gather.12.cloned.1.call-done = bf16[2048,1024]{1,0:T(8,128)(2,1)} async-done(((bf16[256,1024]{1,0:T(8,128)(2,1)}), bf16[2048,1024]{1,0:T(8,128)(2,1)}) %all-gather.12.cloned.1.call-update) | async-done | bytes 4194320 | tf_op jit(solution)/shard_map/all_gather | solution.py:515
  172.9 0.7 collective-permute-start.2
  173.6 4.0 %all-to-all-start.3 = ((bf16[8,256,128]{2,1,0:T(8,128)(2,1)}), bf16[8,256,128]{2,1,0:T(8,128)(2,1)S(1)}, u32[]{:S(2)}, u32[]{:S(2)}) async-start(bf16[8,256,128]{2,1,0:T(8,128)(2,1)} %attention.2), calls=%async_computation.3 | async-start | bytes 1048576 | tf_op jit(solution)/shard_map/all_to_all | solution.py:472
  177.7 0.1 copy.30.accept
  177.8 17.9 %all-to-all-done.3.att = bf16[8,256,128]{2,1,0:T(8,128)(2,1)S(1)} async-done(((bf16[8,256,128]{2,1,0:T(8,128)(2,1)}), bf16[8,256,128]{2,1,0:T(8,128)(2,1)S(1)}, u32[]{:S(2)}, u32[]{:S(2)}) %all-to-all-start.3) | async-done | bytes 524320 | tf_op jit(solution)/shard_map/all_to_all | solution.py:472
  195.7 0.0 collective-permute-done.2.down_b
  195.7 0.0 copy-done.1
  195.7 0.0 copy-start.2
  195.7 0.0 copy-start.3
  195.8 0.0 copy-start.4
  195.8 0.0 copy-start.5
  195.8 11.1 %feed_forward.2.refs_0_.x_ref = bf16[8,256,128]{2,1,0:T(8,128)(2,1)S(1)} custom-call(s32[1]{0:T(128)} %bitcast.column, bf16[8,256,128]{2,1,0:T(8,128)(2,1)S(1)} %all-to-all-done.3.att, bf16[8,256,128]{2,1,0:T(8,128)(2,1)S(1)} %bitcast.71, s32[256,1]{1,0:T(8,128)S(1)} %copy.30.accept, bf16[1024,1024]{1,0:T(8,128)(2,1)} %bitcast.82, ...), custom_call_target="tpu_custom_call" | custom-call | tf_op jit(solution)/shard_map/feed_forward/pallas_call | solution.py:449
  206.9 8.4 %attention.3 = bf16[8,256,128]{2,1,0:T(8,128)(2,1)} custom-call(s32[64]{0:T(128)S(1)} %copy-done.10, s32[1]{0:T(128)} %dynamic_slice.20.length, bf16[8,256,128]{2,1,0:T(8,128)(2,1)S(1)} %feed_forward.2.refs_0_.x_ref, bf16[1024,128]{1,0:T(8,128)(2,1)S(1)} %copy-done.2, bf16[1024,128]{1,0:T(8,128)(2,1)S(1)} %copy-done.3, bf16[1024,128]{1,0:T(8,128)(2,1)S(1)} %copy-done.4, ...), custom_call_target="tpu_custom_call" | custom-call | tf_op jit(solution)/shard_map/attention/pallas_call | solution.py:357
  215.3 3.5 %all-to-all-start.4 = ((bf16[8,256,128]{2,1,0:T(8,128)(2,1)}), bf16[8,256,128]{2,1,0:T(8,128)(2,1)S(1)}, u32[]{:S(2)}, u32[]{:S(2)}) async-start(bf16[8,256,128]{2,1,0:T(8,128)(2,1)} %attention.3), calls=%async_computation.4 | async-start | bytes 1048576 | tf_op jit(solution)/shard_map/all_to_all | solution.py:472
  218.8 0.1 copy.31.accept
  219.0 16.2 %all-to-all-done.4.att = bf16[8,256,128]{2,1,0:T(8,128)(2,1)S(1)} async-done(((bf16[8,256,128]{2,1,0:T(8,128)(2,1)}), bf16[8,256,128]{2,1,0:T(8,128)(2,1)S(1)}, u32[]{:S(2)}, u32[]{:S(2)}) %all-to-all-start.4) | async-done | bytes 524320 | tf_op jit(solution)/shard_map/all_to_all | solution.py:472
  235.1 11.7 %feed_forward.3 = bf16[1,256,128]{2,1,0:T(8,128)(2,1)} custom-call(s32[1]{0:T(128)} %bitcast.column, bf16[8,256,128]{2,1,0:T(8,128)(2,1)S(1)} %all-to-all-done.4.att, bf16[8,256,128]{2,1,0:T(8,128)(2,1)S(1)} %feed_forward.2.refs_0_.x_ref, s32[256,1]{1,0:T(8,128)S(1)} %copy.31.accept, bf16[1024,1024]{1,0:T(8,128)(2,1)} %bitcast.83, ...), custom_call_target="tpu_custom_call" | custom-call | tf_op jit(solution)/shard_map/feed_forward/pallas_call | solution.py:449
  (34 shorter events, 0.2 us)
Async XLA Ops:
  6.5 8.2 %copy-start = (bf16[1024,512]{1,0:T(8,128)(2,1)S(1)}, bf16[1024,512]{1,0:T(8,128)(2,1)}, u32[]{:S(2)}) copy-start(bf16[1024,512]{1,0:T(8,128)(2,1)} %param.25) | copy-start | bytes 3145732
  6.5 77.8 %all-gather.8.cloned.1.call-start = ((), (), s32[]{:S(2)}) async-start(), calls=%async_computation.5 | async-start | bytes 4718592 | tf_op jit(solution)/shard_map/all_gather | solution.py:514
  7.1 8.6 %copy-start.15 = (bf16[128,1024]{1,0:T(8,128)(2,1)S(1)}, bf16[128,1024]{1,0:T(8,128)(2,1)}, u32[]{:S(2)}) copy-start(bf16[128,1024]{1,0:T(8,128)(2,1)} %param.24) | copy-start | bytes 786436
  15.6 97.9 %all-gather.10.cloned.1.call-start = ((), (), s32[]{:S(2)}) async-start(), calls=%async_computation.6 | async-start | bytes 1179648 | tf_op jit(solution)/shard_map/all_gather | solution.py:505
  16.4 8.2 %copy-start.13 = (bf16[512,1024]{1,0:T(8,128)(2,1)S(1)}, bf16[512,1024]{1,0:T(8,128)(2,1)}, u32[]{:S(2)}) copy-start(bf16[512,1024]{1,0:T(8,128)(2,1)} %param.26) | copy-start | bytes 3145732
  16.4 9.1 %copy-start.12 = (s32[32,64]{1,0:T(8,128)S(1)}, s32[32,64]{1,0:T(8,128)}, u32[]{:S(2)}) copy-start(s32[32,64]{1,0:T(8,128)} %page_table.1) | copy-start | bytes 24580
  16.4 13.9 %copy-start.14 = (bf16[256,128]{1,0:T(8,128)(2,1)S(1)}, bf16[256,128]{1,0:T(8,128)(2,1)}, u32[]{:S(2)}) copy-start(bf16[256,128]{1,0:T(8,128)(2,1)} %param.19) | copy-start | bytes 196612
  16.4 62.2 %all-to-all-start.1 = ((bf16[32,2,2,128,128]{4,3,2,1,0:T(8,128)(2,1)}), bf16[32,2,2,128,128]{4,3,2,1,0:T(8,128)(2,1)}, u32[]{:S(2)}, u32[]{:S(2)}) async-start(bf16[32,2,2,128,128]{4,3,2,1,0:T(8,128)(2,1)} %bitcast.90), calls=%async_computation.1 | async-start | bytes 8388608 | tf_op jit(solution)/shard_map/all_to_all | solution.py:198
  24.6 148.4 %all-gather.12.cloned.1.call-start = ((), (), s32[]{:S(2)}) async-start(), calls=%async_computation.7 | async-start | bytes 4718592 | tf_op jit(solution)/shard_map/all_gather | solution.py:515
  78.6 6.7 %copy-start.11 = (bf16[64,128,128]{2,1,0:T(8,128)(2,1)S(1)}, bf16[64,128,128]{2,1,0:T(8,128)(2,1)}, u32[]{:S(2)}) copy-start(bf16[64,128,128]{2,1,0:T(8,128)(2,1)} %keys.1) | copy-start | bytes 6291460
  84.4 62.4 %collective-permute-start = (bf16[8,1024,256]{2,1,0:T(8,128)(2,1)}, bf16[8,1024,256]{2,1,0:T(8,128)(2,1)}, u32[]{:S(2)}, u32[]{:S(2)}) collective-permute-start(bf16[8,1024,256]{2,1,0:T(8,128)(2,1)} %bitcast.84), channel_id=1, source_target_pairs={{0,8},{8,0},{16,24},{24,16},{32,40},{40,32},{48,56},{56,48},{64,72... | collective-permute-start | bytes 12582920 | tf_op jit(solution)/shard_map/ppermute | solution.py:521
  85.3 32.8 %copy-start.18 = (s32[32]{0:T(128)S(1)}, s32[32]{0:T(128)}, u32[]{:S(2)}) copy-start(s32[32]{0:T(128)} %param.33) | copy-start | bytes 388
  85.3 61.5 %all-to-all-start.2 = ((bf16[32,2,2,128,128]{4,3,2,1,0:T(8,128)(2,1)}), bf16[32,2,2,128,128]{4,3,2,1,0:T(8,128)(2,1)}, u32[]{:S(2)}, u32[]{:S(2)}) async-start(bf16[32,2,2,128,128]{4,3,2,1,0:T(8,128)(2,1)} %bitcast.81), calls=%async_computation.2 | async-start | bytes 8388608 | tf_op jit(solution)/shard_map/all_to_all | solution.py:198
  113.5 7.1 %collective-permute-start.1 = (bf16[8,64,1024]{2,1,0:T(8,128)(2,1)}, bf16[8,64,1024]{2,1,0:T(8,128)(2,1)S(1)}, u32[]{:S(2)}, u32[]{:S(2)}) collective-permute-start(bf16[8,64,1024]{2,1,0:T(8,128)(2,1)} %bitcast.91), channel_id=1, source_target_pairs={{0,8},{8,0},{16,24},{24,16},{32,40},{40,32},{48,56},{56,48},{64,72... | collective-permute-start | bytes 3145736 | tf_op jit(solution)/shard_map/ppermute | solution.py:521
  123.9 53.7 %copy-start.17 = (s32[2,256]{1,0:T(2,128)S(1)}, s32[2,256]{1,0:T(2,128)}, u32[]{:S(2)}) copy-start(s32[2,256]{1,0:T(2,128)} %param.35) | copy-start | bytes 6148
  123.9 71.8 %copy-start.1 = (bf16[2048,128]{1,0:T(8,128)(2,1)S(1)}, bf16[2048,128]{1,0:T(8,128)(2,1)}, u32[]{:S(2)}) copy-start(bf16[2048,128]{1,0:T(8,128)(2,1)} %all-gather) | copy-start | bytes 1572868
  123.9 71.8 %copy-start.6 = (f32[1024]{0:T(1024)S(1)}, f32[1024]{0:T(1024)}, u32[]{:S(2)}) copy-start(f32[1024]{0:T(1024)} %param.27) | copy-start | bytes 12292
  123.9 71.8 %copy-start.7 = (f32[1024]{0:T(1024)S(1)}, f32[1024]{0:T(1024)}, u32[]{:S(2)}) copy-start(f32[1024]{0:T(1024)} %param.28) | copy-start | bytes 12292
  123.9 71.8 %copy-start.8 = (f32[1024]{0:T(1024)S(1)}, f32[1024]{0:T(1024)}, u32[]{:S(2)}) copy-start(f32[1024]{0:T(1024)} %param.29) | copy-start | bytes 12292
  123.9 71.8 %copy-start.9 = (f32[1024]{0:T(1024)S(1)}, f32[1024]{0:T(1024)}, u32[]{:S(2)}) copy-start(f32[1024]{0:T(1024)} %param.30) | copy-start | bytes 12292
  172.9 22.8 %collective-permute-start.2 = (bf16[8,256,1024]{2,1,0:T(8,128)(2,1)}, bf16[8,256,1024]{2,1,0:T(8,128)(2,1)}, u32[]{:S(2)}, u32[]{:S(2)}) collective-permute-start(bf16[8,256,1024]{2,1,0:T(8,128)(2,1)} %bitcast.87), channel_id=1, source_target_pairs={{0,8},{8,0},{16,24},{24,16},{32,40},{40,32},{48,56},{56,48},{64,72... | collective-permute-start | bytes 12582920 | tf_op jit(solution)/shard_map/ppermute | solution.py:521
  173.6 22.1 %all-to-all-start.3 = ((bf16[8,256,128]{2,1,0:T(8,128)(2,1)}), bf16[8,256,128]{2,1,0:T(8,128)(2,1)S(1)}, u32[]{:S(2)}, u32[]{:S(2)}) async-start(bf16[8,256,128]{2,1,0:T(8,128)(2,1)} %attention.2), calls=%async_computation.3 | async-start | bytes 1048576 | tf_op jit(solution)/shard_map/all_to_all | solution.py:472
  195.7 11.2 %copy-start.2 = (bf16[1024,128]{1,0:T(8,128)(2,1)S(1)}, bf16[1024,128]{1,0:T(8,128)(2,1)}, u32[]{:S(2)}) copy-start(bf16[1024,128]{1,0:T(8,128)(2,1)} %refs_1_.1) | copy-start | bytes 786436
  195.7 11.2 %copy-start.3 = (bf16[1024,128]{1,0:T(8,128)(2,1)S(1)}, bf16[1024,128]{1,0:T(8,128)(2,1)}, u32[]{:S(2)}) copy-start(bf16[1024,128]{1,0:T(8,128)(2,1)} %refs_2_.1) | copy-start | bytes 786436
  195.8 11.2 %copy-start.4 = (bf16[1024,128]{1,0:T(8,128)(2,1)S(1)}, bf16[1024,128]{1,0:T(8,128)(2,1)}, u32[]{:S(2)}) copy-start(bf16[1024,128]{1,0:T(8,128)(2,1)} %refs_3_.1) | copy-start | bytes 786436
  195.8 11.2 %copy-start.5 = (bf16[1024,128]{1,0:T(8,128)(2,1)S(1)}, bf16[1024,128]{1,0:T(8,128)(2,1)}, u32[]{:S(2)}) copy-start(bf16[1024,128]{1,0:T(8,128)(2,1)} %refs_4_.1) | copy-start | bytes 786436
  195.8 11.2 %copy-start.10 = (s32[64]{0:T(128)S(1)}, s32[64]{0:T(128)}, u32[]{:S(2)}) copy-start(s32[64]{0:T(128)} %compare_select_fusion.1.found) | copy-start | bytes 772
  215.3 19.8 %all-to-all-start.4 = ((bf16[8,256,128]{2,1,0:T(8,128)(2,1)}), bf16[8,256,128]{2,1,0:T(8,128)(2,1)S(1)}, u32[]{:S(2)}, u32[]{:S(2)}) async-start(bf16[8,256,128]{2,1,0:T(8,128)(2,1)} %attention.3), calls=%async_computation.4 | async-start | bytes 1048576 | tf_op jit(solution)/shard_map/all_to_all | solution.py:472
Sparse Core Ops, SparseCore 0:
  15.8 62.6 all-gather.7
  80.3 33.1 all-gather.9
  115.3 57.5 all-gather.11

commit v5 on v4

--- a/solution.py
+++ b/solution.py
@@ -500,18 +500,19 @@
     shard = lax.axis_index("mlp")
     rows, width = embeddings.shape
     core = me % 2
-    half_out = w_out.shape[0] // 2
-    out_half = lax.dynamic_slice_in_dim(w_out, core * half_out, half_out, 0)
-    out_mine = lax.all_gather(out_half, "mlp", axis=0)
-    pages, found, x_parts, (w_up, w_down) = pages_to_owners(
-        page_table, cache_keys, cache_values, (embeddings, w_up, w_down)
+    pages, found, x_parts, (w_up, w_down, w_out) = pages_to_owners(
+        page_table, cache_keys, cache_values, (embeddings, w_up, w_down, w_out)
     )
     length = lax.dynamic_slice_in_dim(lengths, me, 1, 0)
 
     half = w_up.shape[1] // 2
     up_half = lax.dynamic_slice_in_dim(w_up, core * half, half, 1)
     down_half = lax.dynamic_slice_in_dim(w_down, core * half, half, 0)
-    up_mine = lax.all_gather(up_half, "mlp", axis=0)
+    half_out = w_out.shape[0] // 2
+    out_half = lax.dynamic_slice_in_dim(w_out, core * half_out, half_out, 0)
+    blocks = w_out.shape[1] // half
+    out_blocks = [out_half[:, i * half : (i + 1) * half] for i in range(blocks)]
+    up_mine = lax.all_gather(jnp.concatenate([up_half] + out_blocks), "mlp", axis=0)
     down_mine = lax.all_gather(down_half, "mlp", axis=0)
     norms = [v.reshape(1, -1) for v in (norm1_gain, norm1_bias, norm2_gain, norm2_bias)]
     column = shard.reshape(1).astype(jnp.int32)
@@ -520,11 +521,16 @@
     def swap(array):
         return lax.ppermute(array, "pages", core_pair())
 
-    out_other = swap(out_mine)
+    up = (up_mine, swap(up_mine))
+
+    def out_rows(array):
+        tail = array[:, w_up.shape[0] :].reshape(shards, blocks, half_out, half)
+        return jnp.swapaxes(tail, 1, 2).reshape(shards, half_out, w_out.shape[1])
+
+    mine, other = out_rows(up[0]), out_rows(up[1])
     w_out_all = jnp.where(
-        core == 0, jnp.stack([out_mine, out_other], 1), jnp.stack([out_other, out_mine], 1)
-    ).reshape(shards * w_out.shape[0], -1)
-    up = (up_mine, swap(up_mine))
+        core == 0, jnp.stack([mine, other], 1), jnp.stack([other, mine], 1)
+    ).reshape(shards * w_out.shape[0], w_out.shape[1])
     pages, up, w_out_all = lax.optimization_barrier((pages, up, w_out_all))
 
     def layer(outs, attention, x_parts, taken, down):

time: 257 us -> 242 us (0.942); the launches traced: 253 us -> 242 us
  waiting for transfers between devices: 113 us -> 102 us
  local copies, waits for them, and re-layouts: 4.17 us -> 10.8 us
  starting transfers between devices: 29.4 us -> 24.2 us
  other arithmetic: 8.09 us -> 5.22 us
    all_to_all x2, waiting for transfers between devices: 39.7 us -> 61.6 us  [exchange(): lax.all_to_all(pages.reshape((holders, shape[0] // holders) + shape[1:]),...]
    all_gather x1, waiting for transfers between devices: 17.1 us -> 0.02 us  [per_device(): down_mine = lax.all_gather(down_half, 'mlp', axis=0)]
    all_gather x2 -> x1, waiting for transfers between devices: 20.8 us -> 4.45 us  [per_device(): lax.all_gather(jnp.concatenate([up_half] + out_blocks), 'mlp', axis=0)]
    ppermute x3 -> x2, starting transfers between devices: 6.22 us -> 1.66 us  [swap(): return lax.ppermute(array, 'pages', core_pair())]
    select_n x1, other arithmetic: 3.33 us -> 0.34 us  [per_device(): jnp.where(core == 0, jnp.stack([mine, other], 1), jnp.stack([other, mine]...]
    slice x0 -> x2, local copies, waits for them, and re-layouts: none -> 2.59 us  [out_rows(): tail = array[:, w_up.shape[0]:].reshape(shards, blocks, half_out, half)]
  transfers between devices with their start and end apart: 10 -> 8, of which waited for: 7 -> 5; matrix products, arithmetic and copies ran while one was open for 4% -> 6% of each run, Pallas kernels for 7% -> 7%
where the time goes in v5:
time: 242 us
  waiting for transfers between devices  102 us (42%)
  Pallas kernels  56.9 us (24%)
  blocking collectives  28.6 us (12%)
  starting transfers between devices  24.2 us (10%)
  between operations  14.5 us (6%)
  local copies, waits for them, and re-layouts  10.8 us (4%)
  other arithmetic  5.22 us (2%)
    all_to_all x2, waiting for transfers between devices, exchange(): lax.all_to_all(pages.reshape((holders, shape[0] // holders) + shape[1:]),...  61.6 us
    all_to_all x2, waiting for transfers between devices, to_all(): return lax.all_to_all(copies, 'mlp', 0, 0, tiled=True)  35.6 us
    all_gather x1, blocking collectives, pages_to_owners(): x_parts = lax.all_gather(later[0], 'mlp', axis=0)  28.6 us
    pallas_call x2, Pallas kernels, feed_forward(): pl.pallas_call(ffn_kernel, grid=(shards // PER,), out_shape=jax.ShapeDtyp...  22.3 us
    pallas_call x2, Pallas kernels, attend(): pl.pallas_call(functools.partial(attention_kernel, inner), out_shape=jax....  18.3 us
    all_to_all x2, starting transfers between devices, exchange(): lax.all_to_all(pages.reshape((holders, shape[0] // holders) + shape[1:]),...  15 us
    pallas_call x1, Pallas kernels, pack_pages(): pl.pallas_call(pack_kernel, out_shape=jax.ShapeDtypeStruct(shape, BF16),...  7.64 us
    all_to_all x2, starting transfers between devices, to_all(): return lax.all_to_all(copies, 'mlp', 0, 0, tiled=True)  7.52 us
  transfers between devices with their start and end apart: 8, of which 5 were waited for; matrix products, arithmetic and copies ran while one was open for 6% of the time, Pallas kernels for 7%

profile of v5, /device:TPU:9, one launch (start us, length us, event | category | flops | bytes accessed | tf_op | source)
XLA Modules:
  0.0 242.1 jit_solution(14597352086538948548)
XLA Ops:
  6.5 0.0 copy-start
  6.5 0.7 pad_add_fusion.1.where_and_turn
  7.2 7.6 %pack_pages.7 = bf16[64,2,128,128]{3,2,1,0:T(8,128)(2,1)} custom-call(s32[2]{0:T(128)} %pad_add_fusion.1.where_and_turn, s32[32,64]{1,0:T(8,128)} %page_table.1, bf16[64,128,128]{2,1,0:T(8,128)(2,1)} %keys.1, bf16[64,128,128]{2,1,0:T(8,128)(2,1)} %values.1), custom_call_target="tpu_custom_call" | custom-call | tf_op jit(solution)/shard_map/pack_pages/pallas_call | solution.py:166
  15.0 0.8 copy-done.13
  15.9 0.0 all-gather.6.cloned.1.call-update
  15.9 0.0 copy-start.14
  15.9 0.0 copy-start.16
  15.9 7.6 %all-to-all-start.1 = ((bf16[32,2,2,128,128]{4,3,2,1,0:T(8,128)(2,1)}), bf16[32,2,2,128,128]{4,3,2,1,0:T(8,128)(2,1)}, u32[]{:S(2)}, u32[]{:S(2)}) async-start(bf16[32,2,2,128,128]{4,3,2,1,0:T(8,128)(2,1)} %bitcast.91), calls=%async_computation.1 | async-start | bytes 8388608 | tf_op jit(solution)/shard_map/all_to_all | solution.py:198
  23.6 0.0 all-gather.8.cloned.1.call-start
  23.6 0.8 constant_dynamic-slice_fusion
  24.5 0.0 all-gather.8.cloned.1.call-update
  24.6 1.2 convert_reduce_fusion.2
  25.7 0.8 convert_reduce_fusion.3
  26.5 0.3 convert_reduce_fusion
  26.9 0.6 reduce_max.9
  28.2 0.2 convert_reduce_fusion.1
  28.4 0.1 select_reduce_fusion.2
  28.6 0.1 copy.26
  28.7 0.6 sub.64.table
  29.3 28.6 %all-gather = bf16[2048,128]{1,0:T(8,128)(2,1)} all-gather(bf16[256,128]{1,0:T(8,128)(2,1)S(1)} %copy-done.16), channel_id=2, replica_groups=mesh['pages'=32,'mlp'=8] {'mlp'}, dimensions={0}, use_global_device_ids=true | all-gather | bytes 589824 | tf_op jit(solution)/shard_map/all_gather | solution.py:211
  57.9 19.7 %all-to-all-done.1 = bf16[32,2,2,128,128]{4,3,2,1,0:T(8,128)(2,1)} async-done(((bf16[32,2,2,128,128]{4,3,2,1,0:T(8,128)(2,1)}), bf16[32,2,2,128,128]{4,3,2,1,0:T(8,128)(2,1)}, u32[]{:S(2)}, u32[]{:S(2)}) %all-to-all-start.1) | async-done | bytes 4194336 | tf_op jit(solution)/shard_map/all_to_all | solution.py:198
  77.6 6.1 %repack_pages.7 = bf16[64,2,128,128]{3,2,1,0:T(8,128)(2,1)} custom-call(s32[64]{0:T(128)} %sub.64.table, bf16[64,2,128,128]{3,2,1,0:T(8,128)(2,1)} %bitcast.5.got), custom_call_target="tpu_custom_call" | custom-call | tf_op jit(solution)/shard_map/repack_pages/pallas_call | solution.py:184
  83.7 4.4 %all-gather.6.cloned.1.call-done = bf16[10240,256]{1,0:T(8,128)(2,1)} async-done(((bf16[1280,256]{1,0:T(8,128)(2,1)}), bf16[10240,256]{1,0:T(8,128)(2,1)}) %all-gather.6.cloned.1.call-update) | async-done | bytes 5242896 | tf_op jit(solution)/shard_map/all_gather | solution.py:515
  88.1 0.7 collective-permute-start
  88.8 7.4 %all-to-all-start.2 = ((bf16[32,2,2,128,128]{4,3,2,1,0:T(8,128)(2,1)}), bf16[32,2,2,128,128]{4,3,2,1,0:T(8,128)(2,1)}, u32[]{:S(2)}, u32[]{:S(2)}) async-start(bf16[32,2,2,128,128]{4,3,2,1,0:T(8,128)(2,1)} %bitcast.84), calls=%async_computation.2 | async-start | bytes 8388608 | tf_op jit(solution)/shard_map/all_to_all | solution.py:198
  96.2 0.6 dynamic_slice.20.length
  96.8 0.2 convert_reduce_fusion.4
  97.0 0.1 select_reduce_fusion.3
  97.1 0.6 compare_select_fusion.1.found
  97.7 2.7 %project.1 = (bf16[512,128]{1,0:T(8,128)(2,1)}, bf16[512,128]{1,0:T(8,128)(2,1)}, bf16[256,128]{1,0:T(8,128)(2,1)}, bf16[256,128]{1,0:T(8,128)(2,1)}) custom-call(bf16[8,256,128]{2,1,0:T(8,128)(2,1)} %bitcast.73, bf16[1024,128]{1,0:T(8,128)(2,1)} %refs_1_.1, bf16[1024,128]{1,0:T(8,128)(2,1)} %refs_2_.1, bf16[1024,128]{1,0:T(8,128)(2,1)} %refs_3_.1, ...), custom_call_target="tpu_custom_call" | custom-call | tf_op jit(solution)/shard_map/project/pallas_call | solution.py:251
  100.4 1.3 slice.32
  101.7 0.8 copy.35
  102.5 0.8 stack_reshape.8
  103.3 0.0 collective-permute-done.up_b
  103.3 1.3 slice.33
  104.6 0.8 copy.34
  105.4 0.8 stack_reshape.9
  106.2 0.3 maximum_select_fusion
  106.5 0.0 copy-start.19
  106.5 1.6 copy.29
  108.2 0.0 copy-start.10
  108.2 41.9 %all-to-all-done.2 = bf16[32,2,2,128,128]{4,3,2,1,0:T(8,128)(2,1)} async-done(((bf16[32,2,2,128,128]{4,3,2,1,0:T(8,128)(2,1)}), bf16[32,2,2,128,128]{4,3,2,1,0:T(8,128)(2,1)}, u32[]{:S(2)}, u32[]{:S(2)}) %all-to-all-start.2) | async-done | bytes 4194336 | tf_op jit(solution)/shard_map/all_to_all | solution.py:198
  150.1 9.2 %attention.2 = bf16[8,256,128]{2,1,0:T(8,128)(2,1)} custom-call(s32[64]{0:T(128)} %compare_select_fusion.1.found, s32[1]{0:T(128)} %dynamic_slice.20.length, bf16[512,128]{1,0:T(8,128)(2,1)} %get-tuple-element.308.refs_0_, bf16[512,128]{1,0:T(8,128)(2,1)} %get-tuple-element.309.refs_1_, bf16[256,128]{1,0:T(8,128)(2,1)} %get-tuple-element.310.refs_2_, ...), custom_call_target="tpu_custom_call" | custom-call | tf_op jit(solution)/shard_map/attention/pallas_call | solution.py:357
  159.3 0.0 all-gather.8.cloned.1.call-done
  159.3 1.0 collective-permute-start.1
  160.3 4.0 %all-to-all-start.3 = ((bf16[8,256,128]{2,1,0:T(8,128)(2,1)}), bf16[8,256,128]{2,1,0:T(8,128)(2,1)S(1)}, u32[]{:S(2)}, u32[]{:S(2)}) async-start(bf16[8,256,128]{2,1,0:T(8,128)(2,1)} %attention.2), calls=%async_computation.3 | async-start | bytes 1048576 | tf_op jit(solution)/shard_map/all_to_all | solution.py:472
  164.3 0.1 copy.30.accept
  164.5 17.9 %all-to-all-done.3.att = bf16[8,256,128]{2,1,0:T(8,128)(2,1)S(1)} async-done(((bf16[8,256,128]{2,1,0:T(8,128)(2,1)}), bf16[8,256,128]{2,1,0:T(8,128)(2,1)S(1)}, u32[]{:S(2)}, u32[]{:S(2)}) %all-to-all-start.3) | async-done | bytes 524320 | tf_op jit(solution)/shard_map/all_to_all | solution.py:472
  182.3 0.0 collective-permute-done.1.down_b
  182.4 0.0 copy-start.3
  182.4 0.0 copy-start.4
  182.4 0.0 copy-start.5
  182.4 0.0 copy-start.6
  182.4 10.8 %feed_forward.2.refs_0_.x_ref = bf16[8,256,128]{2,1,0:T(8,128)(2,1)S(1)} custom-call(s32[1]{0:T(128)} %bitcast.column, bf16[8,256,128]{2,1,0:T(8,128)(2,1)S(1)} %all-to-all-done.3.att, bf16[8,256,128]{2,1,0:T(8,128)(2,1)S(1)} %bitcast.74, s32[256,1]{1,0:T(8,128)S(1)} %copy.30.accept, bf16[1024,1024]{1,0:T(8,128)(2,1)} %bitcast.89, ...), custom_call_target="tpu_custom_call" | custom-call | tf_op jit(solution)/shard_map/feed_forward/pallas_call | solution.py:449
  193.3 0.0 copy-done.3
  193.3 0.0 copy-done.4
  193.3 0.0 copy-done.5
  193.3 0.0 copy-done.6
  193.3 0.0 copy-done.11
  193.3 9.1 %attention.3 = bf16[8,256,128]{2,1,0:T(8,128)(2,1)} custom-call(s32[64]{0:T(128)S(1)} %copy-done.11, s32[1]{0:T(128)} %dynamic_slice.20.length, bf16[8,256,128]{2,1,0:T(8,128)(2,1)S(1)} %feed_forward.2.refs_0_.x_ref, bf16[1024,128]{1,0:T(8,128)(2,1)S(1)} %copy-done.3, bf16[1024,128]{1,0:T(8,128)(2,1)S(1)} %copy-done.4, bf16[1024,128]{1,0:T(8,128)(2,1)S(1)} %copy-done.5, ...), custom_call_target="tpu_custom_call" | custom-call | tf_op jit(solution)/shard_map/attention/pallas_call | solution.py:357
  202.4 3.5 %all-to-all-start.4 = ((bf16[8,256,128]{2,1,0:T(8,128)(2,1)}), bf16[8,256,128]{2,1,0:T(8,128)(2,1)S(1)}, u32[]{:S(2)}, u32[]{:S(2)}) async-start(bf16[8,256,128]{2,1,0:T(8,128)(2,1)} %attention.3), calls=%async_computation.4 | async-start | bytes 1048576 | tf_op jit(solution)/shard_map/all_to_all | solution.py:472
  205.9 0.1 copy.31.accept
  206.1 17.7 %all-to-all-done.4.att = bf16[8,256,128]{2,1,0:T(8,128)(2,1)S(1)} async-done(((bf16[8,256,128]{2,1,0:T(8,128)(2,1)}), bf16[8,256,128]{2,1,0:T(8,128)(2,1)S(1)}, u32[]{:S(2)}, u32[]{:S(2)}) %all-to-all-start.4) | async-done | bytes 524320 | tf_op jit(solution)/shard_map/all_to_all | solution.py:472
  223.8 11.4 %feed_forward.3 = bf16[1,256,128]{2,1,0:T(8,128)(2,1)} custom-call(s32[1]{0:T(128)} %bitcast.column, bf16[8,256,128]{2,1,0:T(8,128)(2,1)S(1)} %all-to-all-done.4.att, bf16[8,256,128]{2,1,0:T(8,128)(2,1)S(1)} %feed_forward.2.refs_0_.x_ref, s32[256,1]{1,0:T(8,128)S(1)} %copy.31.accept, bf16[1024,1024]{1,0:T(8,128)(2,1)} %bitcast.90, ...), custom_call_target="tpu_custom_call" | custom-call | tf_op jit(solution)/shard_map/feed_forward/pallas_call | solution.py:449
  (43 shorter events, 0.3 us)
Async XLA Ops:
  6.5 17.1 %copy-start = (bf16[512,1024]{1,0:T(8,128)(2,1)S(1)}, bf16[512,1024]{1,0:T(8,128)(2,1)}, u32[]{:S(2)}) copy-start(bf16[512,1024]{1,0:T(8,128)(2,1)} %param.26) | copy-start | bytes 3145732
  6.5 81.6 %all-gather.6.cloned.1.call-start = ((), (), s32[]{:S(2)}) async-start(), calls=%async_computation.5 | async-start | bytes 5898240 | tf_op jit(solution)/shard_map/all_gather | solution.py:515
  7.2 7.7 %copy-start.15 = (bf16[1024,512]{1,0:T(8,128)(2,1)S(1)}, bf16[1024,512]{1,0:T(8,128)(2,1)}, u32[]{:S(2)}) copy-start(bf16[1024,512]{1,0:T(8,128)(2,1)} %param.25) | copy-start | bytes 3145732
  7.2 7.7 %copy-start.17 = (bf16[128,1024]{1,0:T(8,128)(2,1)S(1)}, bf16[128,1024]{1,0:T(8,128)(2,1)}, u32[]{:S(2)}) copy-start(bf16[128,1024]{1,0:T(8,128)(2,1)} %param.24) | copy-start | bytes 786436
  15.0 0.9 copy-start.13
  15.9 8.6 %copy-start.14 = (s32[32,64]{1,0:T(8,128)S(1)}, s32[32,64]{1,0:T(8,128)}, u32[]{:S(2)}) copy-start(s32[32,64]{1,0:T(8,128)} %page_table.1) | copy-start | bytes 24580
  15.9 13.4 %copy-start.16 = (bf16[256,128]{1,0:T(8,128)(2,1)S(1)}, bf16[256,128]{1,0:T(8,128)(2,1)}, u32[]{:S(2)}) copy-start(bf16[256,128]{1,0:T(8,128)(2,1)} %param.19) | copy-start | bytes 196612
  15.9 61.7 %all-to-all-start.1 = ((bf16[32,2,2,128,128]{4,3,2,1,0:T(8,128)(2,1)}), bf16[32,2,2,128,128]{4,3,2,1,0:T(8,128)(2,1)}, u32[]{:S(2)}, u32[]{:S(2)}) async-start(bf16[32,2,2,128,128]{4,3,2,1,0:T(8,128)(2,1)} %bitcast.91), calls=%async_computation.1 | async-start | bytes 8388608 | tf_op jit(solution)/shard_map/all_to_all | solution.py:198
  23.6 135.7 %all-gather.8.cloned.1.call-start = ((), (), s32[]{:S(2)}) async-start(), calls=%async_computation.6 | async-start | bytes 4718592 | tf_op jit(solution)/shard_map/all_gather | solution.py:516
  77.6 11.2 %copy-start.12 = (bf16[64,128,128]{2,1,0:T(8,128)(2,1)S(1)}, bf16[64,128,128]{2,1,0:T(8,128)(2,1)}, u32[]{:S(2)}) copy-start(bf16[64,128,128]{2,1,0:T(8,128)(2,1)} %keys.1) | copy-start | bytes 6291460
  88.1 15.1 %collective-permute-start = (bf16[8,1280,256]{2,1,0:T(8,128)(2,1)}, bf16[8,1280,256]{2,1,0:T(8,128)(2,1)}, u32[]{:S(2)}, u32[]{:S(2)}) collective-permute-start(bf16[8,1280,256]{2,1,0:T(8,128)(2,1)} %bitcast.85), channel_id=1, source_target_pairs={{0,8},{8,0},{16,24},{24,16},{32,40},{40,32},{48,56},{56,48},{64,72... | collective-permute-start | bytes 15728648 | tf_op jit(solution)/shard_map/ppermute | solution.py:522
  88.8 7.4 %copy-start.20 = (s32[32]{0:T(128)S(1)}, s32[32]{0:T(128)}, u32[]{:S(2)}) copy-start(s32[32]{0:T(128)} %param.33) | copy-start | bytes 388
  88.8 61.3 %all-to-all-start.2 = ((bf16[32,2,2,128,128]{4,3,2,1,0:T(8,128)(2,1)}), bf16[32,2,2,128,128]{4,3,2,1,0:T(8,128)(2,1)}, u32[]{:S(2)}, u32[]{:S(2)}) async-start(bf16[32,2,2,128,128]{4,3,2,1,0:T(8,128)(2,1)} %bitcast.84), calls=%async_computation.2 | async-start | bytes 8388608 | tf_op jit(solution)/shard_map/all_to_all | solution.py:198
  106.5 57.8 %copy-start.19 = (s32[2,256]{1,0:T(2,128)S(1)}, s32[2,256]{1,0:T(2,128)}, u32[]{:S(2)}) copy-start(s32[2,256]{1,0:T(2,128)} %param.35) | copy-start | bytes 6148
  108.2 74.2 %copy-start.2 = (bf16[2048,128]{1,0:T(8,128)(2,1)S(1)}, bf16[2048,128]{1,0:T(8,128)(2,1)}, u32[]{:S(2)}) copy-start(bf16[2048,128]{1,0:T(8,128)(2,1)} %all-gather) | copy-start | bytes 1572868
  108.2 74.2 %copy-start.7 = (f32[1024]{0:T(1024)S(1)}, f32[1024]{0:T(1024)}, u32[]{:S(2)}) copy-start(f32[1024]{0:T(1024)} %param.27) | copy-start | bytes 12292
  108.2 74.2 %copy-start.8 = (f32[1024]{0:T(1024)S(1)}, f32[1024]{0:T(1024)}, u32[]{:S(2)}) copy-start(f32[1024]{0:T(1024)} %param.28) | copy-start | bytes 12292
  108.2 74.2 %copy-start.9 = (f32[1024]{0:T(1024)S(1)}, f32[1024]{0:T(1024)}, u32[]{:S(2)}) copy-start(f32[1024]{0:T(1024)} %param.29) | copy-start | bytes 12292
  108.2 74.2 %copy-start.10 = (f32[1024]{0:T(1024)S(1)}, f32[1024]{0:T(1024)}, u32[]{:S(2)}) copy-start(f32[1024]{0:T(1024)} %param.30) | copy-start | bytes 12292
  159.3 23.0 %collective-permute-start.1 = (bf16[8,256,1024]{2,1,0:T(8,128)(2,1)}, bf16[8,256,1024]{2,1,0:T(8,128)(2,1)}, u32[]{:S(2)}, u32[]{:S(2)}) collective-permute-start(bf16[8,256,1024]{2,1,0:T(8,128)(2,1)} %bitcast.92), channel_id=1, source_target_pairs={{0,8},{8,0},{16,24},{24,16},{32,40},{40,32},{48,56},{56,48},{64,72... | collective-permute-start | bytes 12582920 | tf_op jit(solution)/shard_map/ppermute | solution.py:522
  160.3 22.0 %all-to-all-start.3 = ((bf16[8,256,128]{2,1,0:T(8,128)(2,1)}), bf16[8,256,128]{2,1,0:T(8,128)(2,1)S(1)}, u32[]{:S(2)}, u32[]{:S(2)}) async-start(bf16[8,256,128]{2,1,0:T(8,128)(2,1)} %attention.2), calls=%async_computation.3 | async-start | bytes 1048576 | tf_op jit(solution)/shard_map/all_to_all | solution.py:472
  182.4 10.9 %copy-start.3 = (bf16[1024,128]{1,0:T(8,128)(2,1)S(1)}, bf16[1024,128]{1,0:T(8,128)(2,1)}, u32[]{:S(2)}) copy-start(bf16[1024,128]{1,0:T(8,128)(2,1)} %refs_1_.1) | copy-start | bytes 786436
  182.4 10.9 %copy-start.4 = (bf16[1024,128]{1,0:T(8,128)(2,1)S(1)}, bf16[1024,128]{1,0:T(8,128)(2,1)}, u32[]{:S(2)}) copy-start(bf16[1024,128]{1,0:T(8,128)(2,1)} %refs_2_.1) | copy-start | bytes 786436
  182.4 10.9 %copy-start.5 = (bf16[1024,128]{1,0:T(8,128)(2,1)S(1)}, bf16[1024,128]{1,0:T(8,128)(2,1)}, u32[]{:S(2)}) copy-start(bf16[1024,128]{1,0:T(8,128)(2,1)} %refs_3_.1) | copy-start | bytes 786436
  182.4 10.9 %copy-start.6 = (bf16[1024,128]{1,0:T(8,128)(2,1)S(1)}, bf16[1024,128]{1,0:T(8,128)(2,1)}, u32[]{:S(2)}) copy-start(bf16[1024,128]{1,0:T(8,128)(2,1)} %refs_4_.1) | copy-start | bytes 786436
  182.4 10.9 %copy-start.11 = (s32[64]{0:T(128)S(1)}, s32[64]{0:T(128)}, u32[]{:S(2)}) copy-start(s32[64]{0:T(128)} %compare_select_fusion.1.found) | copy-start | bytes 772
  202.4 21.4 %all-to-all-start.4 = ((bf16[8,256,128]{2,1,0:T(8,128)(2,1)}), bf16[8,256,128]{2,1,0:T(8,128)(2,1)S(1)}, u32[]{:S(2)}, u32[]{:S(2)}) async-start(bf16[8,256,128]{2,1,0:T(8,128)(2,1)} %attention.3), calls=%async_computation.4 | async-start | bytes 1048576 | tf_op jit(solution)/shard_map/all_to_all | solution.py:472
  223.8 11.5 %copy-start.1 = (bf16[512,1024]{1,0:T(8,128)(2,1)S(1)}, bf16[512,1024]{1,0:T(8,128)(2,1)}, u32[]{:S(2)}) copy-start(bf16[512,1024]{1,0:T(8,128)(2,1)} %param.26) | copy-start | bytes 3145732
Sparse Core Ops, SparseCore 0:
  16.0 72.0 all-gather.5
  89.9 53.4 all-gather.7
